TPU v7x, 512 devices: a whole 4x8x8 slice. The times are simulated.
512 devices in a mesh: ctx: 64 (over y, z), head: 8 (over x, core).
Axes of the slice: x: 4, y: 8, z: 8, core: 2. Of those that a mesh axis runs over, the one named last changes fastest.
Arguments:
- queries: bfloat16 [8192, 4096], P('ctx', 'head'), may hold values from -45 to 45
- kv_rows: bfloat16 [8192, 512], P('ctx'), may hold values from -6 to 6
- doc_start: int32 [256], replicated, may hold values from 0 to 8160, as said below
- destination: int32 [256], replicated, may hold values from 0 to 255, as said below
- out_weight: bfloat16 [4096, 2048], P('head'), may hold values from -0.5 to 0.5
Outputs:
- mixed: bfloat16 [2048, 8192], P('head', 'ctx')
Inputs may be any that keep to these rules, and one draw needn't show every extreme that they name: Documents are runs of whole blocks: doc_start[b] is a multiple of 32, at most b * 32, never falls from block to block, and equals b * 32 where a document begins; doc_start[0] = 0. `destination`: A permutation of 0 .. 255 that maps every aligned group of 16 consecutive blocks onto itself.
All inputs are finite; a program needn't handle non-finite values.
Results may differ from a plain program's by a relative error of at most 0.011.
Values may be sent and summed in bfloat16 or wider, within the bound.
A program may use at most 64 MiB of HBM per device.

v0:
```python
import jax
import jax.numpy as jnp
import numpy as np
from jax import lax
from jax.sharding import PartitionSpec as P

DH = 128
W1 = 512
W2 = 32
QB = 32
HOPS = 3


def passed_along(block, axis, distance):
    devices = range(lax.axis_size(axis))
    route = [(i - distance, i) for i in devices if i - distance in devices]
    return lax.ppermute(block, axis, route)


def cut_along(x, dim, peers):
    shape = x.shape
    blocks = x.reshape(*shape[:dim], peers, shape[dim] // peers, *shape[dim + 1 :])
    return jnp.moveaxis(blocks, dim, 0)


def summed_on_arrival(x, axis, dim):
    peers = lax.axis_size(axis)
    blocks = lax.all_to_all(cut_along(x, dim, peers), axis, 0, 0, tiled=True)
    return jnp.sum(blocks, axis=0)


def collect_doubling(kv_rows, shards_back, shards_ahead):
    pieces = {0: kv_rows}
    shard_rows = kv_rows.shape[0]
    for direction_sign, wanted in ((1, shards_back), (-1, shards_ahead)):
        held_count = 0
        while held_count < wanted:
            number = min(held_count + 1, wanted - held_count)
            outgoing = jnp.concatenate([pieces[direction_sign * k] for k in range(number)], axis=0)
            incoming = passed_along(outgoing, "ctx", direction_sign * (held_count + 1))
            for k in range(number):
                pieces[direction_sign * (held_count + 1 + k)] = incoming[
                    k * shard_rows : (k + 1) * shard_rows
                ]
            held_count = held_count + number
    return pieces


def attend_block(block_queries, block_id, stacked, base_row, doc_start):
    logit_scale = DH ** (-0.5)
    first_row = block_id * QB
    doc_first = doc_start[block_id]
    window_rows = lax.dynamic_slice_in_dim(stacked, first_row - W1 - base_row, W1 + QB, 0)
    near_rows = lax.dynamic_slice_in_dim(stacked, first_row - W2 + 1 - base_row, QB + W2 - 1, 0)
    keys_first = window_rows[:, :DH]
    values_first = window_rows[:, DH : 2 * DH]
    index_grid = np.arange(QB)[:, None] + np.arange(W2)[None, :]
    keys_second = near_rows[:, 2 * DH : 3 * DH][index_grid]
    values_second = near_rows[:, 3 * DH :][index_grid]
    column_ids = jnp.arange(QB * W2, dtype=jnp.int32)
    query_pos = first_row + column_ids // W2
    second_pos = query_pos - W2 + 1 + column_ids % W2
    column_allowed = second_pos >= doc_first
    tile_rows = W1 // 4
    tail_start = first_row - W1 + QB
    first_tile = jnp.clip((doc_first - tail_start) // tile_rows, 0, 3)

    def allowed_for(key_pos):
        allowed = (key_pos[:, None] >= doc_first) & (key_pos[:, None] <= query_pos[None, :])
        return allowed & (key_pos[:, None] > query_pos[None, :] - W1) & column_allowed[None, :]

    head_allowed = allowed_for(first_row - W1 + jnp.arange(QB, dtype=jnp.int32))
    head_keys = keys_first[:QB]
    head_values = values_first[:QB]
    tail_keys = keys_first[QB:]
    tail_values = values_first[QB:]
    heads_local = block_queries.shape[1] // DH
    per_head = block_queries.reshape(QB, heads_local, DH).transpose(1, 0, 2)

    def one_head(head_query):
        paired = (
            head_query[:, None, :].astype(jnp.float32) * keys_second.astype(jnp.float32)
        ).astype(jnp.bfloat16)
        paired = paired.reshape(QB * W2, DH)

        def scored(keys, allowed):
            values = (
                lax.dot_general(
                    keys, paired, (((1,), (1,)), ((), ())), preferred_element_type=jnp.float32
                )
                * logit_scale
            )
            return jnp.where(allowed, values, jnp.full(values.shape, -jnp.inf, jnp.float32))

        head_logits = scored(head_keys, head_allowed)

        def fill_tile(tile_step, tail):
            tile_keys = lax.dynamic_slice_in_dim(tail_keys, tile_step * tile_rows, tile_rows, 0)
            key_pos = tail_start + tile_step * tile_rows + jnp.arange(tile_rows, dtype=jnp.int32)
            return lax.dynamic_update_slice_in_dim(
                tail, scored(tile_keys, allowed_for(key_pos)), tile_step * tile_rows, 0
            )

        tail_logits = lax.fori_loop(
            first_tile, 4, fill_tile, jnp.full((W1, QB * W2), -jnp.inf, jnp.float32)
        )
        peak = jnp.maximum(head_logits.max(0), tail_logits.max(0)).reshape(QB, W2).max(1)
        repeated = jnp.repeat(peak, W2)[None, :]
        head_weights = jnp.exp(head_logits - repeated)
        tail_weights = jnp.exp(tail_logits - repeated)
        totals = (head_weights.sum(0) + tail_weights.sum(0)).reshape(QB, W2).sum(1)
        head_rounded = head_weights.astype(jnp.bfloat16)
        tail_rounded = tail_weights.astype(jnp.bfloat16)
        start_mix = lax.dot_general(
            head_rounded, head_values, (((0,), (0,)), ((), ())), preferred_element_type=jnp.float32
        )

        def accumulate(tile_step, carried):
            tile_weights = lax.dynamic_slice_in_dim(
                tail_rounded, tile_step * tile_rows, tile_rows, 0
            )
            tile_values = lax.dynamic_slice_in_dim(tail_values, tile_step * tile_rows, tile_rows, 0)
            return carried + lax.dot_general(
                tile_weights,
                tile_values,
                (((0,), (0,)), ((), ())),
                preferred_element_type=jnp.float32,
            )

        mixed_first = lax.fori_loop(first_tile, 4, accumulate, start_mix)
        result = (mixed_first.reshape(QB, W2, DH) * values_second.astype(jnp.float32)).sum(
            1
        ) / totals[:, None]
        return result.astype(jnp.bfloat16)

    outputs = lax.map(one_head, per_head)
    return outputs.transpose(1, 0, 2).reshape(QB, heads_local * DH)


def body(queries, kv_rows, doc_start, destination, out_weight):
    position_ctx = lax.axis_index("ctx")
    tokens_here = queries.shape[0]
    blocks_here = tokens_here // QB
    reach_back = (W1 + tokens_here - 1) // tokens_here
    shards_ahead = 0
    pieces = collect_doubling(kv_rows, reach_back, shards_ahead)
    stacked = jnp.concatenate([pieces[o] for o in range(reach_back, -shards_ahead - 1, -1)], axis=0)
    base_row = (position_ctx - reach_back) * tokens_here
    token_ids = jnp.arange(tokens_here, dtype=jnp.int32)
    same_row = token_ids[:, None] % QB == token_ids[None, :] % QB
    home_blocks = position_ctx * blocks_here + token_ids // QB
    home_targets = destination[home_blocks]
    sources = position_ctx * blocks_here + jnp.arange(blocks_here, dtype=jnp.int32)

    def run_block(inputs):
        return attend_block(inputs[0], inputs[1], stacked, base_row, doc_start)

    attended = lax.map(run_block, (queries.reshape(blocks_here, QB, -1), sources))
    flattened = attended.reshape(tokens_here, -1)
    summed = summed_on_arrival(
        lax.dot_general(
            out_weight, flattened, (((0,), (1,)), ((), ())), preferred_element_type=jnp.float32
        ),
        "head",
        0,
    ).astype(jnp.bfloat16)
    placed = jnp.zeros(summed.shape, jnp.float32)
    for offset in range(-HOPS, HOPS + 1):
        target_slots = (position_ctx + offset) * blocks_here + token_ids // QB
        outgoing = jnp.dot(
            summed,
            ((home_targets[:, None] == target_slots[None, :]) & same_row).astype(jnp.bfloat16),
            preferred_element_type=jnp.float32,
        ).astype(jnp.bfloat16)
        if offset != 0:
            outgoing = passed_along(outgoing, "ctx", offset)
        placed = placed + outgoing.astype(jnp.float32)
    return placed.astype(jnp.bfloat16)


def solution(mesh):
    in_specs = (P("ctx", "head"), P("ctx", None), P(), P(), P("head", None))
    out_specs = P("head", "ctx")
    return jax.shard_map(body, mesh=mesh, in_specs=in_specs, out_specs=out_specs, check_vma=False)
```

profile of v0, /device:TPU:32, one launch (start us, length us, event | category | flops | bytes accessed | tf_op | source)
XLA Modules:
  0.0 535.6 jit_solution(7660752288859008619)
XLA Ops:
  4.4 10.2 %collective-permute-done.1 = bf16[128,512]{1,0:T(8,128)(2,1)S(1)} collective-permute-done((bf16[128,512]{1,0:T(8,128)(2,1)}, bf16[128,512]{1,0:T(8,128)(2,1)S(1)}, u32[]{:S(2)}, u32[]{:S(2)}) %collective-permute-start.1) | collective-permute-done | bytes 131104 | tf_op jit(solution)/shard_map/ppermute | solution.py:17
  17.5 6.1 %collective-permute-start = (bf16[128,512]{1,0:T(8,128)(2,1)}, bf16[128,512]{1,0:T(8,128)(2,1)S(1)}, u32[]{:S(2)}, u32[]{:S(2)}) collective-permute-start(bf16[128,512]{1,0:T(8,128)(2,1)} %param.17), channel_id=1, source_target_pairs={{0,32},{8,40},{16,48},{24,56},{32,64},{40,72},{48,80},{56,88},{64,... | collective-permute-start | bytes 393224 | tf_op jit(solution)/shard_map/ppermute | solution.py:17
  23.6 11.1 %collective-permute-done = bf16[128,512]{1,0:T(8,128)(2,1)S(1)} collective-permute-done((bf16[128,512]{1,0:T(8,128)(2,1)}, bf16[128,512]{1,0:T(8,128)(2,1)S(1)}, u32[]{:S(2)}, u32[]{:S(2)}) %collective-permute-start) | collective-permute-done | bytes 131104 | tf_op jit(solution)/shard_map/ppermute | solution.py:17
  39.3 440.9 %while.88 = (s32[]{:T(128)}, bf16[4,32,512]{2,1,0:T(8,128)(2,1)}, bf16[4,32,512]{2,1,0:T(8,128)(2,1)}, s32[4]{0:T(128)S(1)}, s32[]{:T(128)}, /*index=5*/bf16[640...) while((s32[]{:T(128)}, bf16[4,32,512]{2,1,0:T(8,128)(2,1)}, ...), condition=%wide.region_14.15_spmd.clone.clone, body=%wide.region_0.14_spmd.sunk.clone.clone.sunk | while | flops 88274392 | bytes 14309076 | solution.py:158
  56.7 92.1 %while.89 = (s32[]{:T(128)}, bf16[4,32,128]{2,1,0:T(8,128)(2,1)S(1)}, bf16[4,32,128]{2,1,0:T(8,128)(2,1)S(1)}, bf16[32,32,128]{2,1,0:T(8,128)(2,1)S(1)}, bf16[32...) while((s32[]{:T(128)}, ...), condition=%wide.region_13.13_spmd.clone.clone, body=%wide.region_1.12_spmd.clone.clone.sunk | while | flops 88246608 | bytes 12218415 | solution.py:136
  59.0 9.8 %while.90 = (s32[]{:T(128)}, f32[512,1024]{1,0:T(8,128)}, s32[]{:T(128)}, s32[]{:T(128)}, s32[1024]{0:T(1024)S(1)}, /*index=5*/pred[1024]{0:T(1024)(128)(4,1)S(1...) while((s32[]{:T(128)}, f32[512,1024]{1,0:T(8,128)}, ...), condition=%wide.region_4.3_spmd, body=%wide.region_3.2_spmd.sunk | while | flops 34473352 | bytes 839099 | solution.py:104
  82.0 9.8 %while.90 = (s32[]{:T(128)}, f32[512,1024]{1,0:T(8,128)}, s32[]{:T(128)}, s32[]{:T(128)}, s32[1024]{0:T(1024)S(1)}, /*index=5*/pred[1024]{0:T(1024)(128)(4,1)S(1...) while((s32[]{:T(128)}, f32[512,1024]{1,0:T(8,128)}, ...), condition=%wide.region_4.3_spmd, body=%wide.region_3.2_spmd.sunk | while | flops 34473352 | bytes 839099 | solution.py:104
  105.0 9.8 %while.90 = (s32[]{:T(128)}, f32[512,1024]{1,0:T(8,128)}, s32[]{:T(128)}, s32[]{:T(128)}, s32[1024]{0:T(1024)S(1)}, /*index=5*/pred[1024]{0:T(1024)(128)(4,1)S(1...) while((s32[]{:T(128)}, f32[512,1024]{1,0:T(8,128)}, ...), condition=%wide.region_4.3_spmd, body=%wide.region_3.2_spmd.sunk | while | flops 34473352 | bytes 839099 | solution.py:104
  128.1 9.8 %while.90 = (s32[]{:T(128)}, f32[512,1024]{1,0:T(8,128)}, s32[]{:T(128)}, s32[]{:T(128)}, s32[1024]{0:T(1024)S(1)}, /*index=5*/pred[1024]{0:T(1024)(128)(4,1)S(1...) while((s32[]{:T(128)}, f32[512,1024]{1,0:T(8,128)}, ...), condition=%wide.region_4.3_spmd, body=%wide.region_3.2_spmd.sunk | while | flops 34473352 | bytes 839099 | solution.py:104
  143.6 5.0 while.91
  166.9 92.1 %while.89 = (s32[]{:T(128)}, bf16[4,32,128]{2,1,0:T(8,128)(2,1)S(1)}, bf16[4,32,128]{2,1,0:T(8,128)(2,1)S(1)}, bf16[32,32,128]{2,1,0:T(8,128)(2,1)S(1)}, bf16[32...) while((s32[]{:T(128)}, ...), condition=%wide.region_13.13_spmd.clone.clone, body=%wide.region_1.12_spmd.clone.clone.sunk | while | flops 88246608 | bytes 12218415 | solution.py:136
  169.2 9.8 %while.90 = (s32[]{:T(128)}, f32[512,1024]{1,0:T(8,128)}, s32[]{:T(128)}, s32[]{:T(128)}, s32[1024]{0:T(1024)S(1)}, /*index=5*/pred[1024]{0:T(1024)(128)(4,1)S(1...) while((s32[]{:T(128)}, f32[512,1024]{1,0:T(8,128)}, ...), condition=%wide.region_4.3_spmd, body=%wide.region_3.2_spmd.sunk | while | flops 34473352 | bytes 839099 | solution.py:104
  192.2 9.8 %while.90 = (s32[]{:T(128)}, f32[512,1024]{1,0:T(8,128)}, s32[]{:T(128)}, s32[]{:T(128)}, s32[1024]{0:T(1024)S(1)}, /*index=5*/pred[1024]{0:T(1024)(128)(4,1)S(1...) while((s32[]{:T(128)}, f32[512,1024]{1,0:T(8,128)}, ...), condition=%wide.region_4.3_spmd, body=%wide.region_3.2_spmd.sunk | while | flops 34473352 | bytes 839099 | solution.py:104
  215.3 9.8 %while.90 = (s32[]{:T(128)}, f32[512,1024]{1,0:T(8,128)}, s32[]{:T(128)}, s32[]{:T(128)}, s32[1024]{0:T(1024)S(1)}, /*index=5*/pred[1024]{0:T(1024)(128)(4,1)S(1...) while((s32[]{:T(128)}, f32[512,1024]{1,0:T(8,128)}, ...), condition=%wide.region_4.3_spmd, body=%wide.region_3.2_spmd.sunk | while | flops 34473352 | bytes 839099 | solution.py:104
  230.8 5.0 while.91
  238.3 9.8 %while.90 = (s32[]{:T(128)}, f32[512,1024]{1,0:T(8,128)}, s32[]{:T(128)}, s32[]{:T(128)}, s32[1024]{0:T(1024)S(1)}, /*index=5*/pred[1024]{0:T(1024)(128)(4,1)S(1...) while((s32[]{:T(128)}, f32[512,1024]{1,0:T(8,128)}, ...), condition=%wide.region_4.3_spmd, body=%wide.region_3.2_spmd.sunk | while | flops 34473352 | bytes 839099 | solution.py:104
  253.8 5.0 while.91
  277.2 92.1 %while.89 = (s32[]{:T(128)}, bf16[4,32,128]{2,1,0:T(8,128)(2,1)S(1)}, bf16[4,32,128]{2,1,0:T(8,128)(2,1)S(1)}, bf16[32,32,128]{2,1,0:T(8,128)(2,1)S(1)}, bf16[32...) while((s32[]{:T(128)}, ...), condition=%wide.region_13.13_spmd.clone.clone, body=%wide.region_1.12_spmd.clone.clone.sunk | while | flops 88246608 | bytes 12218415 | solution.py:136
  279.4 9.8 %while.90 = (s32[]{:T(128)}, f32[512,1024]{1,0:T(8,128)}, s32[]{:T(128)}, s32[]{:T(128)}, s32[1024]{0:T(1024)S(1)}, /*index=5*/pred[1024]{0:T(1024)(128)(4,1)S(1...) while((s32[]{:T(128)}, f32[512,1024]{1,0:T(8,128)}, ...), condition=%wide.region_4.3_spmd, body=%wide.region_3.2_spmd.sunk | while | flops 34473352 | bytes 839099 | solution.py:104
  302.5 9.8 %while.90 = (s32[]{:T(128)}, f32[512,1024]{1,0:T(8,128)}, s32[]{:T(128)}, s32[]{:T(128)}, s32[1024]{0:T(1024)S(1)}, /*index=5*/pred[1024]{0:T(1024)(128)(4,1)S(1...) while((s32[]{:T(128)}, f32[512,1024]{1,0:T(8,128)}, ...), condition=%wide.region_4.3_spmd, body=%wide.region_3.2_spmd.sunk | while | flops 34473352 | bytes 839099 | solution.py:104
  318.0 5.0 while.91
  325.5 9.8 %while.90 = (s32[]{:T(128)}, f32[512,1024]{1,0:T(8,128)}, s32[]{:T(128)}, s32[]{:T(128)}, s32[1024]{0:T(1024)S(1)}, /*index=5*/pred[1024]{0:T(1024)(128)(4,1)S(1...) while((s32[]{:T(128)}, f32[512,1024]{1,0:T(8,128)}, ...), condition=%wide.region_4.3_spmd, body=%wide.region_3.2_spmd.sunk | while | flops 34473352 | bytes 839099 | solution.py:104
  348.5 9.8 %while.90 = (s32[]{:T(128)}, f32[512,1024]{1,0:T(8,128)}, s32[]{:T(128)}, s32[]{:T(128)}, s32[1024]{0:T(1024)S(1)}, /*index=5*/pred[1024]{0:T(1024)(128)(4,1)S(1...) while((s32[]{:T(128)}, f32[512,1024]{1,0:T(8,128)}, ...), condition=%wide.region_4.3_spmd, body=%wide.region_3.2_spmd.sunk | while | flops 34473352 | bytes 839099 | solution.py:104
  387.4 92.1 %while.89 = (s32[]{:T(128)}, bf16[4,32,128]{2,1,0:T(8,128)(2,1)S(1)}, bf16[4,32,128]{2,1,0:T(8,128)(2,1)S(1)}, bf16[32,32,128]{2,1,0:T(8,128)(2,1)S(1)}, bf16[32...) while((s32[]{:T(128)}, ...), condition=%wide.region_13.13_spmd.clone.clone, body=%wide.region_1.12_spmd.clone.clone.sunk | while | flops 88246608 | bytes 12218415 | solution.py:136
  389.7 9.8 %while.90 = (s32[]{:T(128)}, f32[512,1024]{1,0:T(8,128)}, s32[]{:T(128)}, s32[]{:T(128)}, s32[1024]{0:T(1024)S(1)}, /*index=5*/pred[1024]{0:T(1024)(128)(4,1)S(1...) while((s32[]{:T(128)}, f32[512,1024]{1,0:T(8,128)}, ...), condition=%wide.region_4.3_spmd, body=%wide.region_3.2_spmd.sunk | while | flops 34473352 | bytes 839099 | solution.py:104
  412.7 9.8 %while.90 = (s32[]{:T(128)}, f32[512,1024]{1,0:T(8,128)}, s32[]{:T(128)}, s32[]{:T(128)}, s32[1024]{0:T(1024)S(1)}, /*index=5*/pred[1024]{0:T(1024)(128)(4,1)S(1...) while((s32[]{:T(128)}, f32[512,1024]{1,0:T(8,128)}, ...), condition=%wide.region_4.3_spmd, body=%wide.region_3.2_spmd.sunk | while | flops 34473352 | bytes 839099 | solution.py:104
  435.7 9.8 %while.90 = (s32[]{:T(128)}, f32[512,1024]{1,0:T(8,128)}, s32[]{:T(128)}, s32[]{:T(128)}, s32[1024]{0:T(1024)S(1)}, /*index=5*/pred[1024]{0:T(1024)(128)(4,1)S(1...) while((s32[]{:T(128)}, f32[512,1024]{1,0:T(8,128)}, ...), condition=%wide.region_4.3_spmd, body=%wide.region_3.2_spmd.sunk | while | flops 34473352 | bytes 839099 | solution.py:104
  458.8 9.8 %while.90 = (s32[]{:T(128)}, f32[512,1024]{1,0:T(8,128)}, s32[]{:T(128)}, s32[]{:T(128)}, s32[1024]{0:T(1024)S(1)}, /*index=5*/pred[1024]{0:T(1024)(128)(4,1)S(1...) while((s32[]{:T(128)}, f32[512,1024]{1,0:T(8,128)}, ...), condition=%wide.region_4.3_spmd, body=%wide.region_3.2_spmd.sunk | while | flops 34473352 | bytes 839099 | solution.py:104
  488.4 14.5 %all-to-all-done = f32[8,256,128]{1,2,0:T(8,128)S(1)} async-done(((f32[8,256,128]{1,2,0:T(8,128)}), f32[8,256,128]{1,2,0:T(8,128)S(1)}, u32[]{:S(2)}, u32[]{:S(2)}) %all-to-all-start) | async-done | bytes 1048608 | tf_op jit(solution)/shard_map/all_to_all | solution.py:28
  505.4 5.5 %collective-permute-start.4 = (bf16[256,128]{1,0:T(8,128)(2,1)S(1)}, bf16[256,128]{1,0:T(8,128)(2,1)S(1)}, u32[]{:S(2)}, u32[]{:S(2)}) collective-permute-start(bf16[256,128]{1,0:T(8,128)(2,1)S(1)} %convolution_convert_fusion.5), channel_id=1, source_target_pairs={{16,0},{24,8},{32,16},{40,24},{48,32},{56,40},{64,48},{72,56},{80,... | collective-permute-start | bytes 196616 | tf_op jit(solution)/shard_map/ppermute | solution.py:17
  511.1 5.8 %collective-permute-start.5 = (bf16[256,128]{1,0:T(8,128)(2,1)S(1)}, bf16[256,128]{1,0:T(8,128)(2,1)S(1)}, u32[]{:S(2)}, u32[]{:S(2)}) collective-permute-start(bf16[256,128]{1,0:T(8,128)(2,1)S(1)} %convolution_convert_fusion.4), channel_id=1, source_target_pairs={{8,0},{16,8},{24,16},{32,24},{40,32},{48,40},{56,48},{64,56},{72,6... | collective-permute-start | bytes 196616 | tf_op jit(solution)/shard_map/ppermute | solution.py:17
  521.5 5.9 %collective-permute-start.8 = (bf16[256,128]{1,0:T(8,128)(2,1)S(1)}, bf16[256,128]{1,0:T(8,128)(2,1)S(1)}, u32[]{:S(2)}, u32[]{:S(2)}) collective-permute-start(bf16[256,128]{1,0:T(8,128)(2,1)S(1)} %convolution_convert_fusion), channel_id=1, source_target_pairs={{0,24},{8,32},{16,40},{24,48},{32,56},{40,64},{48,72},{56,80},{64,... | collective-permute-start | bytes 196616 | tf_op jit(solution)/shard_map/ppermute | solution.py:17
  (774 shorter events, 518.1 us)
Async XLA Ops:
  0.0 480.2 %copy-start = (bf16[512,2048]{1,0:T(8,128)(2,1)S(1)}, bf16[512,2048]{1,0:T(8,128)(2,1)}, u32[]{:S(2)}) copy-start(bf16[512,2048]{1,0:T(8,128)(2,1)} %param.20) | copy-start | bytes 6291460
  0.0 14.7 %collective-permute-start.1 = (bf16[128,512]{1,0:T(8,128)(2,1)}, bf16[128,512]{1,0:T(8,128)(2,1)S(1)}, u32[]{:S(2)}, u32[]{:S(2)}) collective-permute-start(bf16[128,512]{1,0:T(8,128)(2,1)} %param.17), channel_id=1, source_target_pairs={{0,8},{8,16},{16,24},{24,32},{32,40},{40,48},{48,56},{56,64},{64,7... | collective-permute-start | bytes 393224 | tf_op jit(solution)/shard_map/ppermute | solution.py:17
  15.6 20.2 %collective-permute-start.2 = (bf16[256,512]{1,0:T(8,128)(2,1)S(1)}, bf16[256,512]{1,0:T(8,128)(2,1)S(1)}, u32[]{:S(2)}, u32[]{:S(2)}) collective-permute-start(bf16[256,512]{1,0:T(8,128)(2,1)S(1)} %pad_maximum_fusion), channel_id=1, source_target_pairs={{0,16},{8,24},{16,32},{24,40},{32,48},{40,56},{48,64},{56,72},{64,... | collective-permute-start | bytes 786440 | tf_op jit(solution)/shard_map/ppermute | solution.py:17
  17.5 17.3 %collective-permute-start = (bf16[128,512]{1,0:T(8,128)(2,1)}, bf16[128,512]{1,0:T(8,128)(2,1)S(1)}, u32[]{:S(2)}, u32[]{:S(2)}) collective-permute-start(bf16[128,512]{1,0:T(8,128)(2,1)} %param.17), channel_id=1, source_target_pairs={{0,32},{8,40},{16,48},{24,56},{32,64},{40,72},{48,80},{56,88},{64,... | collective-permute-start | bytes 393224 | tf_op jit(solution)/shard_map/ppermute | solution.py:17
  481.6 5.4 %copy-start.1 = (s32[256]{0:T(256)S(1)}, s32[256]{0:T(256)}, u32[]{:S(2)}) copy-start(s32[256]{0:T(256)} %param.19) | copy-start | bytes 3076
  482.7 20.2 %all-to-all-start = ((f32[8,256,128]{1,2,0:T(8,128)}), f32[8,256,128]{1,2,0:T(8,128)S(1)}, u32[]{:S(2)}, u32[]{:S(2)}) async-start(f32[8,256,128]{1,2,0:T(8,128)} %bitcast.76), calls=%async_computation | async-start | bytes 2097152 | tf_op jit(solution)/shard_map/all_to_all | solution.py:28
  503.2 18.3 %collective-permute-start.3 = (bf16[256,128]{1,0:T(8,128)(2,1)S(1)}, bf16[256,128]{1,0:T(8,128)(2,1)S(1)}, u32[]{:S(2)}, u32[]{:S(2)}) collective-permute-start(bf16[256,128]{1,0:T(8,128)(2,1)S(1)} %convolution_convert_fusion.6), channel_id=1, source_target_pairs={{24,0},{32,8},{40,16},{48,24},{56,32},{64,40},{72,48},{80,56},{88,... | collective-permute-start | bytes 196616 | tf_op jit(solution)/shard_map/ppermute | solution.py:17
  505.4 22.1 %collective-permute-start.4 = (bf16[256,128]{1,0:T(8,128)(2,1)S(1)}, bf16[256,128]{1,0:T(8,128)(2,1)S(1)}, u32[]{:S(2)}, u32[]{:S(2)}) collective-permute-start(bf16[256,128]{1,0:T(8,128)(2,1)S(1)} %convolution_convert_fusion.5), channel_id=1, source_target_pairs={{16,0},{24,8},{32,16},{40,24},{48,32},{56,40},{64,48},{72,56},{80,... | collective-permute-start | bytes 196616 | tf_op jit(solution)/shard_map/ppermute | solution.py:17
  511.1 16.4 %collective-permute-start.5 = (bf16[256,128]{1,0:T(8,128)(2,1)S(1)}, bf16[256,128]{1,0:T(8,128)(2,1)S(1)}, u32[]{:S(2)}, u32[]{:S(2)}) collective-permute-start(bf16[256,128]{1,0:T(8,128)(2,1)S(1)} %convolution_convert_fusion.4), channel_id=1, source_target_pairs={{8,0},{16,8},{24,16},{32,24},{40,32},{48,40},{56,48},{64,56},{72,6... | collective-permute-start | bytes 196616 | tf_op jit(solution)/shard_map/ppermute | solution.py:17
  517.1 10.6 %collective-permute-start.6 = (bf16[256,128]{1,0:T(8,128)(2,1)S(1)}, bf16[256,128]{1,0:T(8,128)(2,1)S(1)}, u32[]{:S(2)}, u32[]{:S(2)}) collective-permute-start(bf16[256,128]{1,0:T(8,128)(2,1)S(1)} %convolution_convert_fusion.2), channel_id=1, source_target_pairs={{0,8},{8,16},{16,24},{24,32},{32,40},{40,48},{48,56},{56,64},{64,7... | collective-permute-start | bytes 196616 | tf_op jit(solution)/shard_map/ppermute | solution.py:17
  519.3 10.5 %collective-permute-start.7 = (bf16[256,128]{1,0:T(8,128)(2,1)S(1)}, bf16[256,128]{1,0:T(8,128)(2,1)S(1)}, u32[]{:S(2)}, u32[]{:S(2)}) collective-permute-start(bf16[256,128]{1,0:T(8,128)(2,1)S(1)} %convolution_convert_fusion.1), channel_id=1, source_target_pairs={{0,16},{8,24},{16,32},{24,40},{32,48},{40,56},{48,64},{56,72},{64,... | collective-permute-start | bytes 196616 | tf_op jit(solution)/shard_map/ppermute | solution.py:17
  521.5 13.2 %collective-permute-start.8 = (bf16[256,128]{1,0:T(8,128)(2,1)S(1)}, bf16[256,128]{1,0:T(8,128)(2,1)S(1)}, u32[]{:S(2)}, u32[]{:S(2)}) collective-permute-start(bf16[256,128]{1,0:T(8,128)(2,1)S(1)} %convolution_convert_fusion), channel_id=1, source_target_pairs={{0,24},{8,32},{16,40},{24,48},{32,56},{40,64},{48,72},{56,80},{64,... | collective-permute-start | bytes 196616 | tf_op jit(solution)/shard_map/ppermute | solution.py:17
where the time goes:
time: 546 us; the launch traced here: 536 us
  matrix products  209 us (38%)
  other arithmetic  136 us (25%)
  local copies, waits for them, and re-layouts  88.6 us (16%)
  waiting for transfers between devices  43.4 us (8%)
  starting transfers between devices  39.7 us (7%)
  loops' own time  18.1 us (3%)
    dot_general x80, matrix products, scored(): lax.dot_general(keys, paired, (((1,), (1,)), ((), ())), preferred_element...  123 us
    dot_general x64, matrix products, accumulate(): lax.dot_general(tile_weights, tile_values, (((0,), (0,)), ((), ())), pref...  78.2 us
    reduce_sum x48, other arithmetic, one_head(): totals = (head_weights.sum(0) + tail_weights.sum(0)).reshape(QB, W2).sum(1)  49.1 us
    ge x68, other arithmetic, allowed_for(): key_pos[:, None] >= doc_first  37.5 us
    ppermute x9, starting transfers between devices, passed_along(): return lax.ppermute(block, axis, route)  35.4 us
    ppermute x9, waiting for transfers between devices, passed_along(): return lax.ppermute(block, axis, route)  28.9 us
    reduce_max x16, other arithmetic, one_head(): tail_logits.max(0)  27.8 us
    another operation x16, local copies, waits for them, and re-layouts  25.8 us
  transfers between devices with their start and end apart: 10, of which 7 were waited for; matrix products, arithmetic and copies ran while one was open for 1% of the time, Pallas kernels for 0%

commit v1 on v0

v1 whole, which is shorter than its diff:
```python
import jax
import jax.numpy as jnp
from jax import lax
from jax.experimental import pallas as pl
from jax.experimental.pallas import tpu as pltpu
from jax.sharding import PartitionSpec as P

DH = 128
W1 = 512
W2 = 32
QB = 32
HOPS = 3
CS = DH**-0.5 * 1.4426950408889634
BIG = -1e30

def passed_along(block, axis, distance):
    devices = range(lax.axis_size(axis))
    route = [(i - distance, i) for i in devices if i - distance in devices]
    return lax.ppermute(block, axis, route)


def cut_along(x, dim, peers):
    shape = x.shape
    blocks = x.reshape(*shape[:dim], peers, shape[dim] // peers, *shape[dim + 1 :])
    return jnp.moveaxis(blocks, dim, 0)


def summed_on_arrival(x, axis, dim):
    peers = lax.axis_size(axis)
    blocks = lax.all_to_all(cut_along(x, dim, peers), axis, 0, 0, tiled=True)
    return jnp.sum(blocks, axis=0)


def collect_doubling(kv_rows, shards_back, shards_ahead):
    pieces = {0: kv_rows}
    shard_rows = kv_rows.shape[0]
    for direction_sign, wanted in ((1, shards_back), (-1, shards_ahead)):
        held_count = 0
        while held_count < wanted:
            number = min(held_count + 1, wanted - held_count)
            outgoing = jnp.concatenate([pieces[direction_sign * k] for k in range(number)], axis=0)
            incoming = passed_along(outgoing, "ctx", direction_sign * (held_count + 1))
            for k in range(number):
                pieces[direction_sign * (held_count + 1 + k)] = incoming[
                    k * shard_rows : (k + 1) * shard_rows
                ]
            held_count = held_count + number
    return pieces


def prep(kvw_ref, near_ref, dstart, base, k1x, v1t, k2x, v2x, k2f, v2t):
    k1x[:, :DH] = kvw_ref[:, :DH]
    row = lax.broadcasted_iota(jnp.int32,(640,DH),0)//QB
    col = lax.broadcasted_iota(jnp.int32,(640,DH),1)
    oh = jnp.where((row==col)|(col==32),1.0,0.0)
    k1x[:, DH:] = oh.astype(jnp.bfloat16)
    v = kvw_ref[:, DH:2*DH].astype(jnp.float32)
    v1t[:DH,:] = v.T.astype(jnp.bfloat16)
    v1t[DH:,:] = jnp.ones((16,640),jnp.bfloat16)
    nf = near_ref[...].astype(jnp.float32)
    k2f[...] = nf[:, :DH]
    vt = nf[:, DH:].T
    v2t[:, :160] = vt
    v2t[:, 160:] = jnp.zeros((DH,96),jnp.float32)
    t = lax.broadcasted_iota(jnp.int32,(128,DH),0)
    c = lax.broadcasted_iota(jnp.int32,(128,DH),1)
    s = jnp.where(t<32, dstart[0], jnp.where(t<64, dstart[1], jnp.where(t<96,dstart[2],dstart[3]))) - base
    keymask = (c<20) & ((c*QB - W1) < s)
    for m in range(W2):
        k2x[m,:, :DH] = k2f[m+1:m+129, :].astype(jnp.bfloat16)
        mm = (c==32) & ((t-31+m) < s)
        k2x[m,:, DH:] = jnp.where(keymask|mm, BIG, 0.0).astype(jnp.bfloat16)
        full = v2t[...]
        r = pltpu.roll(full, 256-(m+1), 1)
        v2x[m] = r[:, :128]

def attn_kernel(dstart_ref, base_ref, q_ref, kvw_ref, near_ref, out_ref, k1x, v1t, k2x, v2x, k2f, v2t, s0, s1, acc):
    prep(kvw_ref, near_ref, [dstart_ref[i] for i in range(4)], base_ref[0], k1x, v1t, k2x, v2x, k2f, v2t)
    jj = lax.broadcasted_iota(jnp.int32,(128,256),0)
    tt = lax.broadcasted_iota(jnp.int32,(128,256),1)%128
    first = jj > tt
    H=4; NP=W2//2
    def scores(h, mp, sref):
        q = q_ref[:, pl.ds(pl.multiple_of(h*DH,DH),DH)]
        rhs=[]
        for u in range(2):
            m = 31-(2*mp+u)
            p = q*k2x[m,:, :DH]
            rhs.append(jnp.concatenate([p, k2x[m,:,DH:]],axis=1))
        rhs = jnp.concatenate(rhs,axis=0)
        s = lax.dot_general(k1x[...], rhs, (((1,),(1,)),((),())), preferred_element_type=jnp.float32)
        sref[0:128,:] = jnp.where(first, s[:128], s[512:])
        sref[128:512,:] = s[128:512]
    def proc(h, mp, sref, M, L):
        s = sref[...]
        cm = s.max(axis=0,keepdims=True)
        Mn = jnp.maximum(M, jnp.maximum(cm[:, :128],cm[:,128:]))
        al = jnp.exp2((M-Mn)*CS)
        Mc = jnp.concatenate([Mn,Mn],axis=1)
        p = jnp.exp2((s-Mc)*CS).astype(jnp.bfloat16)
        pm = p[:128]
        z = jnp.zeros_like(pm)
        pf = jnp.concatenate([jnp.where(first,pm,z), p[128:], jnp.where(first,z,pm)],axis=0)
        o = jnp.dot(v1t[...], pf, preferred_element_type=jnp.float32)
        m = 31-2*mp
        acc[...] = acc[...]*al + o[:DH,:128]*v2x[m] + o[:DH,128:]*v2x[m-1]
        L = L*al + o[DH:DH+1,:128] + o[DH:DH+1,128:]
        return Mn, L
    def head(h, _):
        acc[...] = jnp.zeros_like(acc)
        M = jnp.full((1,128),BIG,jnp.float32); L=jnp.zeros((1,128),jnp.float32)
        scores(h,0,s0)
        def body(k, c):
            M,L=c
            scores(h,2*k+1,s1)
            M,L = proc(h,2*k,s0,M,L)
            scores(h,jnp.minimum(2*k+2,NP-1),s0)
            M,L = proc(h,2*k+1,s1,M,L)
            return M,L
        M,L = lax.fori_loop(0,NP//2,body,(M,L))
        r = acc[...]/L
        out_ref[:, pl.ds(pl.multiple_of(h*DH,DH),DH)] = r.T.astype(jnp.bfloat16)
        return 0
    lax.fori_loop(0,H,head,0)

def attention(dstart4, base, q, kvw, near):
    V=pl.BlockSpec(memory_space=pltpu.VMEM); S=pl.BlockSpec(memory_space=pltpu.SMEM)
    return pl.pallas_call(attn_kernel, out_shape=jax.ShapeDtypeStruct((128,512),jnp.bfloat16),
        in_specs=[S,S,V,V,V], out_specs=V,
        scratch_shapes=[pltpu.VMEM((640,256),jnp.bfloat16), pltpu.VMEM((144,640),jnp.bfloat16),
          pltpu.VMEM((32,128,256),jnp.bfloat16), pltpu.VMEM((32,128,128),jnp.float32),
          pltpu.VMEM((160,128),jnp.float32), pltpu.VMEM((128,256),jnp.float32),
          pltpu.VMEM((512,256),jnp.float32), pltpu.VMEM((512,256),jnp.float32), pltpu.VMEM((128,128),jnp.float32)],
        compiler_params=pltpu.CompilerParams(vmem_limit_bytes=60*2**20),
    )(dstart4, base, q, kvw, near)


def body(queries, kv_rows, doc_start, destination, out_weight):
    position_ctx = lax.axis_index("ctx")
    tokens_here = queries.shape[0]
    blocks_here = tokens_here // QB
    reach_back = (W1 + tokens_here - 1) // tokens_here
    shards_ahead = 0
    pieces = collect_doubling(kv_rows, reach_back, shards_ahead)
    stacked = jnp.concatenate([pieces[o] for o in range(reach_back, -shards_ahead - 1, -1)], axis=0)
    token_ids = jnp.arange(tokens_here, dtype=jnp.int32)
    same_row = token_ids[:, None] % QB == token_ids[None, :] % QB
    home_blocks = position_ctx * blocks_here + token_ids // QB
    home_targets = destination[home_blocks]

    first_block = position_ctx * blocks_here
    starts = lax.dynamic_slice_in_dim(doc_start, first_block, blocks_here, 0)
    base = (position_ctx * tokens_here).reshape(1)
    flattened = attention(starts, base, queries, stacked[:, : 2 * DH], stacked[W1 - W2 :, 2 * DH :])
    summed = summed_on_arrival(
        lax.dot_general(
            out_weight, flattened, (((0,), (1,)), ((), ())), preferred_element_type=jnp.float32
        ),
        "head",
        0,
    ).astype(jnp.bfloat16)
    placed = jnp.zeros(summed.shape, jnp.float32)
    for offset in range(-HOPS, HOPS + 1):
        target_slots = (position_ctx + offset) * blocks_here + token_ids // QB
        outgoing = jnp.dot(
            summed,
            ((home_targets[:, None] == target_slots[None, :]) & same_row).astype(jnp.bfloat16),
            preferred_element_type=jnp.float32,
        ).astype(jnp.bfloat16)
        if offset != 0:
            outgoing = passed_along(outgoing, "ctx", offset)
        placed = placed + outgoing.astype(jnp.float32)
    return placed.astype(jnp.bfloat16)


def solution(mesh):
    in_specs = (P("ctx", "head"), P("ctx", None), P(), P(), P("head", None))
    out_specs = P("head", "ctx")
    return jax.shard_map(body, mesh=mesh, in_specs=in_specs, out_specs=out_specs, check_vma=False)
```

time: 546 us -> 123 us (0.23)
  the two profiles are of different devices: /device:TPU:32 before, /device:TPU:96 now
where the time goes in v1:
time: 123 us; the launch traced here: 122 us
  starting transfers between devices  53 us (43%)
  waiting for transfers between devices  30.4 us (25%)
  Pallas kernels  26.8 us (22%)
  local copies, waits for them, and re-layouts  5.33 us (4%)
  matrix products  3.67 us (3%)
  other arithmetic  2.52 us (2%)
    ppermute x9, starting transfers between devices, passed_along(): return lax.ppermute(block, axis, route)  48.7 us
    pallas_call x1, Pallas kernels, attention(): pl.pallas_call(attn_kernel, out_shape=jax.ShapeDtypeStruct((128, 512), jn...  26.8 us
    ppermute x9, waiting for transfers between devices, passed_along(): return lax.ppermute(block, axis, route)  15.9 us
    all_to_all x1, waiting for transfers between devices, summed_on_arrival(): blocks = lax.all_to_all(cut_along(x, dim, peers), axis, 0, 0, tiled=True)  14.5 us
    all_to_all x1, starting transfers between devices, summed_on_arrival(): blocks = lax.all_to_all(cut_along(x, dim, peers), axis, 0, 0, tiled=True)  4.28 us
  transfers between devices with their start and end apart: 10, of which 5 were waited for; matrix products, arithmetic and copies ran while one was open for 4% of the time, Pallas kernels for 0%

profile of v1, /device:TPU:96, one launch (start us, length us, event | category | flops | bytes accessed | tf_op | source)
XLA Modules:
  0.0 122.0 jit_solution(3616799998611275674)
XLA Ops:
  0.0 4.4 %collective-permute-start.1 = (bf16[128,512]{1,0:T(8,128)(2,1)}, bf16[128,512]{1,0:T(8,128)(2,1)S(1)}, u32[]{:S(2)}, u32[]{:S(2)}) collective-permute-start(bf16[128,512]{1,0:T(8,128)(2,1)} %param.6), channel_id=1, source_target_pairs={{0,8},{8,16},{16,24},{24,32},{32,40},{40,48},{48,56},{56,64},{64,7... | collective-permute-start | bytes 393224 | tf_op jit(solution)/shard_map/ppermute | solution.py:19
  4.4 3.1 %collective-permute-done.1 = bf16[128,512]{1,0:T(8,128)(2,1)S(1)} collective-permute-done((bf16[128,512]{1,0:T(8,128)(2,1)}, bf16[128,512]{1,0:T(8,128)(2,1)S(1)}, u32[]{:S(2)}, u32[]{:S(2)}) %collective-permute-start.1) | collective-permute-done | bytes 131104 | tf_op jit(solution)/shard_map/ppermute | solution.py:19
  7.5 0.9 pad_maximum_fusion
  8.4 7.3 %collective-permute-start.2 = (bf16[256,512]{1,0:T(8,128)(2,1)S(1)}, bf16[256,512]{1,0:T(8,128)(2,1)S(1)}, u32[]{:S(2)}, u32[]{:S(2)}) collective-permute-start(bf16[256,512]{1,0:T(8,128)(2,1)S(1)} %pad_maximum_fusion), channel_id=1, source_target_pairs={{0,16},{8,24},{16,32},{24,40},{32,48},{40,56},{48,64},{56,72},{64,... | collective-permute-start | bytes 786440 | tf_op jit(solution)/shard_map/ppermute | solution.py:19
  15.7 7.0 %collective-permute-start = (bf16[128,512]{1,0:T(8,128)(2,1)}, bf16[128,512]{1,0:T(8,128)(2,1)S(1)}, u32[]{:S(2)}, u32[]{:S(2)}) collective-permute-start(bf16[128,512]{1,0:T(8,128)(2,1)} %param.6), channel_id=1, source_target_pairs={{0,32},{8,40},{16,48},{24,56},{32,64},{40,72},{48,80},{56,88},{64,... | collective-permute-start | bytes 393224 | tf_op jit(solution)/shard_map/ppermute | solution.py:19
  22.7 1.3 %dynamic_slice.3.dstart_ref = s32[4]{0:T(128)} dynamic-slice(s32[256]{0:T(256)} %param.7, s32[]{:T(128)S(6)} %select_n.101), dynamic_slice_sizes={4} | dynamic-slice | bytes 36 | tf_op jit(solution)/shard_map/dynamic_slice | solution.py:152
  24.0 1.5 %pad_maximum_fusion.1.near_ref = bf16[160,256]{1,0:T(8,128)(2,1)} fusion(bf16[128,512]{1,0:T(8,128)(2,1)} %param.6, bf16[128,512]{1,0:T(8,128)(2,1)S(1)} %collective-permute-done.1), kind=kLoop, calls=%fused_computation.21 | loop fusion | flops 163840 | bytes 344064 | tf_op jit(solution)/shard_map/concatenate | solution.py:145
  25.5 4.2 %collective-permute-done = bf16[128,512]{1,0:T(8,128)(2,1)S(1)} collective-permute-done((bf16[128,512]{1,0:T(8,128)(2,1)}, bf16[128,512]{1,0:T(8,128)(2,1)S(1)}, u32[]{:S(2)}, u32[]{:S(2)}) %collective-permute-start) | collective-permute-done | bytes 131104 | tf_op jit(solution)/shard_map/ppermute | solution.py:19
  29.8 0.9 constant_dynamic-update-slice_fusion
  30.7 0.8 slice.21.kvw_ref
  31.5 26.8 %shard_map.55 = bf16[128,512]{1,0:T(8,128)(2,1)} custom-call(s32[4]{0:T(128)} %dynamic_slice.3.dstart_ref, s32[1]{0:T(128)} %bitcast.base_ref, bf16[128,512]{1,0:T(8,128)(2,1)} %q_ref.1, bf16[640,256]{1,0:T(8,128)(2,1)} %slice.21.kvw_ref, bf16[160,256]{1,0:T(8,128)(2,1)} %pad_maximum_fusion.1.near_ref), custom_call_target="tpu_custom_call" | custom-call | tf_op jit(solution)/shard_map/pallas_call | solution.py:128
  58.3 1.3 %fusion.39 = f32[128,2048]{1,0:T(8,128)S(1)} fusion(bf16[128,512]{1,0:T(8,128)(2,1)} %shard_map.55, bf16[512,2048]{1,0:T(8,128)(2,1)S(1)} %copy-done), kind=kOutput, calls=%fused_computation.80 | convolution fusion | flops 268435456 | bytes 3276800 | tf_op jit(solution)/shard_map/dot_general | solution.py:156
  59.6 1.1 copy.11
  60.7 4.3 %all-to-all-start = ((f32[8,256,128]{1,2,0:T(8,128)}), f32[8,256,128]{1,2,0:T(8,128)S(1)}, u32[]{:S(2)}, u32[]{:S(2)}) async-start(f32[8,256,128]{1,2,0:T(8,128)} %bitcast.18), calls=%async_computation | async-start | bytes 2097152 | tf_op jit(solution)/shard_map/all_to_all | solution.py:30
  65.0 1.3 %gather_fusion = s32[128]{0:T(128)S(1)} fusion(s32[256]{0:T(256)S(1)} %copy-done.1, s32[1024]{0:T(1024)S(1)} %pad_clamp_fusion), kind=kCustom, calls=%fused_computation | custom fusion | bytes 1536 | tf_op jit(solution)/shard_map/gather | solution.py:149
  66.4 14.5 %all-to-all-done = f32[8,256,128]{1,2,0:T(8,128)S(1)} async-done(((f32[8,256,128]{1,2,0:T(8,128)}), f32[8,256,128]{1,2,0:T(8,128)S(1)}, u32[]{:S(2)}, u32[]{:S(2)}) %all-to-all-start) | async-done | bytes 1048608 | tf_op jit(solution)/shard_map/all_to_all | solution.py:30
  80.9 0.1 reduce_sum.9
  81.0 0.2 convolution_convert_fusion.6
  81.2 10.8 %collective-permute-start.3 = (bf16[256,128]{1,0:T(8,128)(2,1)S(1)}, bf16[256,128]{1,0:T(8,128)(2,1)S(1)}, u32[]{:S(2)}, u32[]{:S(2)}) collective-permute-start(bf16[256,128]{1,0:T(8,128)(2,1)S(1)} %convolution_convert_fusion.6), channel_id=1, source_target_pairs={{24,0},{32,8},{40,16},{48,24},{56,32},{64,40},{72,48},{80,56},{88,... | collective-permute-start | bytes 196616 | tf_op jit(solution)/shard_map/ppermute | solution.py:19
  92.0 0.2 convolution_convert_fusion.5
  92.3 4.5 %collective-permute-start.4 = (bf16[256,128]{1,0:T(8,128)(2,1)S(1)}, bf16[256,128]{1,0:T(8,128)(2,1)S(1)}, u32[]{:S(2)}, u32[]{:S(2)}) collective-permute-start(bf16[256,128]{1,0:T(8,128)(2,1)S(1)} %convolution_convert_fusion.5), channel_id=1, source_target_pairs={{16,0},{24,8},{32,16},{40,24},{48,32},{56,40},{64,48},{72,56},{80,... | collective-permute-start | bytes 196616 | tf_op jit(solution)/shard_map/ppermute | solution.py:19
  96.8 0.2 convolution_convert_fusion.4
  97.1 1.9 %collective-permute-start.5 = (bf16[256,128]{1,0:T(8,128)(2,1)S(1)}, bf16[256,128]{1,0:T(8,128)(2,1)S(1)}, u32[]{:S(2)}, u32[]{:S(2)}) collective-permute-start(bf16[256,128]{1,0:T(8,128)(2,1)S(1)} %convolution_convert_fusion.4), channel_id=1, source_target_pairs={{8,0},{16,8},{24,16},{32,24},{40,32},{48,40},{56,48},{64,56},{72,6... | collective-permute-start | bytes 196616 | tf_op jit(solution)/shard_map/ppermute | solution.py:19
  99.0 0.2 convolution_convert_fusion.2
  99.2 3.9 %collective-permute-start.6 = (bf16[256,128]{1,0:T(8,128)(2,1)S(1)}, bf16[256,128]{1,0:T(8,128)(2,1)S(1)}, u32[]{:S(2)}, u32[]{:S(2)}) collective-permute-start(bf16[256,128]{1,0:T(8,128)(2,1)S(1)} %convolution_convert_fusion.2), channel_id=1, source_target_pairs={{0,8},{8,16},{16,24},{24,32},{32,40},{40,48},{48,56},{56,64},{64,7... | collective-permute-start | bytes 196616 | tf_op jit(solution)/shard_map/ppermute | solution.py:19
  103.2 0.2 convolution_convert_fusion.1
  103.4 5.5 %collective-permute-start.7 = (bf16[256,128]{1,0:T(8,128)(2,1)S(1)}, bf16[256,128]{1,0:T(8,128)(2,1)S(1)}, u32[]{:S(2)}, u32[]{:S(2)}) collective-permute-start(bf16[256,128]{1,0:T(8,128)(2,1)S(1)} %convolution_convert_fusion.1), channel_id=1, source_target_pairs={{0,16},{8,24},{16,32},{24,40},{32,48},{40,56},{48,64},{56,72},{64,... | collective-permute-start | bytes 196616 | tf_op jit(solution)/shard_map/ppermute | solution.py:19
  108.9 0.2 convolution_convert_fusion
  109.1 3.4 %collective-permute-start.8 = (bf16[256,128]{1,0:T(8,128)(2,1)S(1)}, bf16[256,128]{1,0:T(8,128)(2,1)S(1)}, u32[]{:S(2)}, u32[]{:S(2)}) collective-permute-start(bf16[256,128]{1,0:T(8,128)(2,1)S(1)} %convolution_convert_fusion), channel_id=1, source_target_pairs={{0,24},{8,32},{16,40},{24,48},{32,56},{40,64},{48,72},{56,80},{64,... | collective-permute-start | bytes 196616 | tf_op jit(solution)/shard_map/ppermute | solution.py:19
  112.6 1.5 %collective-permute-done.7 = bf16[256,128]{1,0:T(8,128)(2,1)S(1)} collective-permute-done((bf16[256,128]{1,0:T(8,128)(2,1)S(1)}, bf16[256,128]{1,0:T(8,128)(2,1)S(1)}, u32[]{:S(2)}, u32[]{:S(2)}) %collective-permute-start.7) | collective-permute-done | bytes 65568 | tf_op jit(solution)/shard_map/ppermute | solution.py:19
  114.0 7.1 %collective-permute-done.8 = bf16[256,128]{1,0:T(8,128)(2,1)S(1)} collective-permute-done((bf16[256,128]{1,0:T(8,128)(2,1)S(1)}, bf16[256,128]{1,0:T(8,128)(2,1)S(1)}, u32[]{:S(2)}, u32[]{:S(2)}) %collective-permute-start.8) | collective-permute-done | bytes 65568 | tf_op jit(solution)/shard_map/ppermute | solution.py:19
  121.1 0.9 add_convert_fusion
  (23 shorter events, 0.1 us)
Async XLA Ops:
  0.0 58.3 %copy-start = (bf16[512,2048]{1,0:T(8,128)(2,1)S(1)}, bf16[512,2048]{1,0:T(8,128)(2,1)}, u32[]{:S(2)}) copy-start(bf16[512,2048]{1,0:T(8,128)(2,1)} %param.9) | copy-start | bytes 6291460
  0.0 7.5 %collective-permute-start.1 = (bf16[128,512]{1,0:T(8,128)(2,1)}, bf16[128,512]{1,0:T(8,128)(2,1)S(1)}, u32[]{:S(2)}, u32[]{:S(2)}) collective-permute-start(bf16[128,512]{1,0:T(8,128)(2,1)} %param.6), channel_id=1, source_target_pairs={{0,8},{8,16},{16,24},{24,32},{32,40},{40,48},{48,56},{56,64},{64,7... | collective-permute-start | bytes 393224 | tf_op jit(solution)/shard_map/ppermute | solution.py:19
  8.4 21.3 %collective-permute-start.2 = (bf16[256,512]{1,0:T(8,128)(2,1)S(1)}, bf16[256,512]{1,0:T(8,128)(2,1)S(1)}, u32[]{:S(2)}, u32[]{:S(2)}) collective-permute-start(bf16[256,512]{1,0:T(8,128)(2,1)S(1)} %pad_maximum_fusion), channel_id=1, source_target_pairs={{0,16},{8,24},{16,32},{24,40},{32,48},{40,56},{48,64},{56,72},{64,... | collective-permute-start | bytes 786440 | tf_op jit(solution)/shard_map/ppermute | solution.py:19
  15.7 14.0 %collective-permute-start = (bf16[128,512]{1,0:T(8,128)(2,1)}, bf16[128,512]{1,0:T(8,128)(2,1)S(1)}, u32[]{:S(2)}, u32[]{:S(2)}) collective-permute-start(bf16[128,512]{1,0:T(8,128)(2,1)} %param.6), channel_id=1, source_target_pairs={{0,32},{8,40},{16,48},{24,56},{32,64},{40,72},{48,80},{56,88},{64,... | collective-permute-start | bytes 393224 | tf_op jit(solution)/shard_map/ppermute | solution.py:19
  59.6 5.4 %copy-start.1 = (s32[256]{0:T(256)S(1)}, s32[256]{0:T(256)}, u32[]{:S(2)}) copy-start(s32[256]{0:T(256)} %param.8) | copy-start | bytes 3076
  60.7 20.2 %all-to-all-start = ((f32[8,256,128]{1,2,0:T(8,128)}), f32[8,256,128]{1,2,0:T(8,128)S(1)}, u32[]{:S(2)}, u32[]{:S(2)}) async-start(f32[8,256,128]{1,2,0:T(8,128)} %bitcast.18), calls=%async_computation | async-start | bytes 2097152 | tf_op jit(solution)/shard_map/all_to_all | solution.py:30
  81.2 27.9 %collective-permute-start.3 = (bf16[256,128]{1,0:T(8,128)(2,1)S(1)}, bf16[256,128]{1,0:T(8,128)(2,1)S(1)}, u32[]{:S(2)}, u32[]{:S(2)}) collective-permute-start(bf16[256,128]{1,0:T(8,128)(2,1)S(1)} %convolution_convert_fusion.6), channel_id=1, source_target_pairs={{24,0},{32,8},{40,16},{48,24},{56,32},{64,40},{72,48},{80,56},{88,... | collective-permute-start | bytes 196616 | tf_op jit(solution)/shard_map/ppermute | solution.py:19
  92.3 20.3 %collective-permute-start.4 = (bf16[256,128]{1,0:T(8,128)(2,1)S(1)}, bf16[256,128]{1,0:T(8,128)(2,1)S(1)}, u32[]{:S(2)}, u32[]{:S(2)}) collective-permute-start(bf16[256,128]{1,0:T(8,128)(2,1)S(1)} %convolution_convert_fusion.5), channel_id=1, source_target_pairs={{16,0},{24,8},{32,16},{40,24},{48,32},{56,40},{64,48},{72,56},{80,... | collective-permute-start | bytes 196616 | tf_op jit(solution)/shard_map/ppermute | solution.py:19
  97.1 15.5 %collective-permute-start.5 = (bf16[256,128]{1,0:T(8,128)(2,1)S(1)}, bf16[256,128]{1,0:T(8,128)(2,1)S(1)}, u32[]{:S(2)}, u32[]{:S(2)}) collective-permute-start(bf16[256,128]{1,0:T(8,128)(2,1)S(1)} %convolution_convert_fusion.4), channel_id=1, source_target_pairs={{8,0},{16,8},{24,16},{32,24},{40,32},{48,40},{56,48},{64,56},{72,6... | collective-permute-start | bytes 196616 | tf_op jit(solution)/shard_map/ppermute | solution.py:19
  99.2 13.3 %collective-permute-start.6 = (bf16[256,128]{1,0:T(8,128)(2,1)S(1)}, bf16[256,128]{1,0:T(8,128)(2,1)S(1)}, u32[]{:S(2)}, u32[]{:S(2)}) collective-permute-start(bf16[256,128]{1,0:T(8,128)(2,1)S(1)} %convolution_convert_fusion.2), channel_id=1, source_target_pairs={{0,8},{8,16},{16,24},{24,32},{32,40},{40,48},{48,56},{56,64},{64,7... | collective-permute-start | bytes 196616 | tf_op jit(solution)/shard_map/ppermute | solution.py:19
  103.4 10.6 %collective-permute-start.7 = (bf16[256,128]{1,0:T(8,128)(2,1)S(1)}, bf16[256,128]{1,0:T(8,128)(2,1)S(1)}, u32[]{:S(2)}, u32[]{:S(2)}) collective-permute-start(bf16[256,128]{1,0:T(8,128)(2,1)S(1)} %convolution_convert_fusion.1), channel_id=1, source_target_pairs={{0,16},{8,24},{16,32},{24,40},{32,48},{40,56},{48,64},{56,72},{64,... | collective-permute-start | bytes 196616 | tf_op jit(solution)/shard_map/ppermute | solution.py:19
  109.1 12.0 %collective-permute-start.8 = (bf16[256,128]{1,0:T(8,128)(2,1)S(1)}, bf16[256,128]{1,0:T(8,128)(2,1)S(1)}, u32[]{:S(2)}, u32[]{:S(2)}) collective-permute-start(bf16[256,128]{1,0:T(8,128)(2,1)S(1)} %convolution_convert_fusion), channel_id=1, source_target_pairs={{0,24},{8,32},{16,40},{24,48},{32,56},{40,64},{48,72},{56,80},{64,... | collective-permute-start | bytes 196616 | tf_op jit(solution)/shard_map/ppermute | solution.py:19

commit v2 on v1

--- a/solution.py
+++ b/solution.py
@@ -9,43 +9,120 @@
 W1 = 512
 W2 = 32
 QB = 32
-HOPS = 3
+GROUP = 4
 CS = DH**-0.5 * 1.4426950408889634
 BIG = -1e30
 
-def passed_along(block, axis, distance):
-    devices = range(lax.axis_size(axis))
-    route = [(i - distance, i) for i in devices if i - distance in devices]
-    return lax.ppermute(block, axis, route)
-
-
-def cut_along(x, dim, peers):
-    shape = x.shape
-    blocks = x.reshape(*shape[:dim], peers, shape[dim] // peers, *shape[dim + 1 :])
-    return jnp.moveaxis(blocks, dim, 0)
-
-
-def summed_on_arrival(x, axis, dim):
-    peers = lax.axis_size(axis)
-    blocks = lax.all_to_all(cut_along(x, dim, peers), axis, 0, 0, tiled=True)
-    return jnp.sum(blocks, axis=0)
-
-
-def collect_doubling(kv_rows, shards_back, shards_ahead):
-    pieces = {0: kv_rows}
-    shard_rows = kv_rows.shape[0]
-    for direction_sign, wanted in ((1, shards_back), (-1, shards_ahead)):
-        held_count = 0
-        while held_count < wanted:
-            number = min(held_count + 1, wanted - held_count)
-            outgoing = jnp.concatenate([pieces[direction_sign * k] for k in range(number)], axis=0)
-            incoming = passed_along(outgoing, "ctx", direction_sign * (held_count + 1))
-            for k in range(number):
-                pieces[direction_sign * (held_count + 1 + k)] = incoming[
-                    k * shard_rows : (k + 1) * shard_rows
-                ]
-            held_count = held_count + number
-    return pieces
+
+def remote(src, dst, ssem, rsem, ctx, head):
+    return pltpu.make_async_remote_copy(src_ref=src, dst_ref=dst, send_sem=ssem, recv_sem=rsem,
+        device_id=(ctx, head), device_id_type=pl.DeviceIdType.MESH)
+
+def gather_kernel(kv_ref, kvw_ref, near_ref, send1, recv1, send2, recv2, near_sems):
+    c = lax.axis_index("ctx"); e = lax.axis_index("head")
+    nc = lax.axis_size("ctx"); nh = lax.axis_size("head")
+    rows = kv_ref.shape[0]; piece = rows//nh; back = W1//rows
+    barrier = pltpu.get_barrier_semaphore()
+    for d in range(1, back+1):
+        pl.semaphore_signal(barrier, inc=1, device_id=(lax.rem(c+nc-d,nc), e), device_id_type=pl.DeviceIdType.MESH)
+    for k in range(1, nh):
+        pl.semaphore_signal(barrier, inc=1, device_id=(c, lax.rem(e+k,nh)), device_id_type=pl.DeviceIdType.MESH)
+    own = pl.ds(pl.multiple_of(e*piece, piece), piece)
+    kvw_ref[W1:, :] = kv_ref[:, :2*DH]
+    near_ref[W2:, :] = kv_ref[:, 2*DH:]
+    pl.semaphore_wait(barrier, back+nh-1)
+    def slot(d, h):
+        return kvw_ref.at[pl.ds(pl.multiple_of((back-d)*rows+h*piece, piece), piece), :]
+    first=[]
+    for d in range(1, back+1):
+        cp = remote(kv_ref.at[own, pl.ds(0,2*DH)], slot(d,e), send1.at[d-1], recv1.at[d-1], lax.rem(c+d,nc), e)
+        cp.start(); first.append(cp)
+        if d==1:
+            near = remote(kv_ref.at[pl.ds(rows-W2,W2), pl.ds(2*DH,2*DH)], near_ref.at[pl.ds(0,W2),:], near_sems.at[0], near_sems.at[1], lax.rem(c+1,nc), e)
+            near.start()
+    second=[]
+    for d in range(1, back+1):
+        first[d-1].wait_recv()
+        for k in range(1, nh):
+            cp = remote(slot(d,e), slot(d,e), send2.at[d-1,k-1], recv2.at[d-1,k-1], c, lax.rem(e+k,nh))
+            cp.start(); second.append(cp)
+    for cp in first: cp.wait_send()
+    near.wait()
+    for cp in second: cp.wait()
+
+def gather_kv(kv_rows, nh):
+    rows = kv_rows.shape[0]; back=W1//rows
+    V=pl.BlockSpec(memory_space=pltpu.VMEM)
+    D=pltpu.SemaphoreType.DMA
+    return pl.pallas_call(gather_kernel,
+        out_shape=(jax.ShapeDtypeStruct((W1+rows,2*DH),jnp.bfloat16), jax.ShapeDtypeStruct((W2+rows,2*DH),jnp.bfloat16)),
+        in_specs=[V], out_specs=(V,V),
+        scratch_shapes=[D((back,)),D((back,)),D((back,nh-1)),D((back,nh-1)),D((2,))],
+        compiler_params=pltpu.CompilerParams(collective_id=0, has_side_effects=True))(kv_rows)
+
+def tail_kernel(dest_ref, att_ref, w_ref, out_ref, part, got, mine, grp, ssem, rsem, gs, gr):
+    c = lax.axis_index("ctx"); e = lax.axis_index("head")
+    nh = lax.axis_size("head")
+    tokens = att_ref.shape[0]; nb = tokens//QB; feats = out_ref.shape[0]
+    pos = lax.rem(c, GROUP); g0 = c - pos
+    barrier = pltpu.get_barrier_semaphore()
+    for k in range(1, nh):
+        pl.semaphore_signal(barrier, inc=1, device_id=(c, lax.rem(e+k,nh)), device_id_type=pl.DeviceIdType.MESH)
+    for k in range(1, GROUP):
+        pl.semaphore_signal(barrier, inc=1, device_id=(g0+lax.rem(pos+k,GROUP), e), device_id_type=pl.DeviceIdType.MESH)
+    def project(h):
+        return jnp.dot(att_ref[...], w_ref[:, pl.ds(pl.multiple_of(h*feats,feats),feats)], preferred_element_type=jnp.float32)
+    sends=[]
+    for k in [4,3,5,2,6,1,7][:nh-1] if nh==8 else range(1,nh):
+        h = lax.rem(e+k,nh)
+        part[k-1] = project(h).astype(jnp.bfloat16).reshape(nb,QB,feats)
+        if not sends:
+            pl.semaphore_wait(barrier, nh-1+GROUP-1)
+        for b in range(nb):
+            cp = remote(part.at[k-1,b], got.at[k-1,b], ssem.at[k-1,b], rsem.at[k-1,b], c, h)
+            cp.start(); sends.append((k,b,cp))
+    own = project(e).reshape(nb,QB,feats)
+    by = {(k,b):cp for k,b,cp in sends}
+    gsends=[]
+    for b in range(nb):
+        total = own[b]
+        for k in range(1,nh):
+            by[(k,b)].wait_recv()
+        for k in range(1,nh):
+            total = total + got[k-1,b].astype(jnp.float32)
+        mine[b] = total.astype(jnp.bfloat16)
+        for k in range(1,GROUP):
+            cp = remote(mine.at[b], grp.at[k-1,b], gs.at[k-1,b], gr.at[k-1,b], g0+lax.rem(pos+k,GROUP), e)
+            cp.start(); gsends.append(cp)
+    rows=[]
+    idx=[]
+    for s in range(nb):
+        found = jnp.int32(0)
+        for j in range(GROUP*nb):
+            found = jnp.where(dest_ref[g0*nb+j]==c*nb+s, j, found)
+        idx.append(found)
+    for cp in gsends: cp.wait_recv()
+    for s in range(nb):
+        src = lax.div(idx[s], nb); b = lax.rem(idx[s], nb)
+        k = lax.rem(pos - src + GROUP, GROUP)
+        far = grp[jnp.maximum(k-1,0), b].astype(jnp.float32)
+        near = mine[b].astype(jnp.float32)
+        rows.append(jnp.where(k==0, near, far))
+    full = jnp.concatenate(rows, axis=0)
+    out_ref[...] = full.T.astype(jnp.bfloat16)
+    for _,_,cp in sends: cp.wait_send()
+    for cp in gsends: cp.wait_send()
+
+def tail(destination, att, w, nh):
+    tokens=att.shape[0]; nb=tokens//QB; feats=w.shape[1]//nh
+    V=pl.BlockSpec(memory_space=pltpu.VMEM); S=pl.BlockSpec(memory_space=pltpu.SMEM)
+    D=pltpu.SemaphoreType.DMA
+    return pl.pallas_call(tail_kernel, out_shape=jax.ShapeDtypeStruct((feats,tokens),jnp.bfloat16),
+        in_specs=[S,V,V], out_specs=V,
+        scratch_shapes=[pltpu.VMEM((nh-1,nb,QB,feats),jnp.bfloat16), pltpu.VMEM((nh-1,nb,QB,feats),jnp.bfloat16),
+            pltpu.VMEM((nb,QB,feats),jnp.bfloat16), pltpu.VMEM((GROUP-1,nb,QB,feats),jnp.bfloat16),
+            D((nh-1,nb)),D((nh-1,nb)),D((GROUP-1,nb)),D((GROUP-1,nb))],
+        compiler_params=pltpu.CompilerParams(collective_id=1, has_side_effects=True, vmem_limit_bytes=40*2**20))(destination, att, w)
 
 
 def prep(kvw_ref, near_ref, dstart, base, k1x, v1t, k2x, v2x, k2f, v2t):
@@ -139,38 +216,12 @@
     position_ctx = lax.axis_index("ctx")
     tokens_here = queries.shape[0]
     blocks_here = tokens_here // QB
-    reach_back = (W1 + tokens_here - 1) // tokens_here
-    shards_ahead = 0
-    pieces = collect_doubling(kv_rows, reach_back, shards_ahead)
-    stacked = jnp.concatenate([pieces[o] for o in range(reach_back, -shards_ahead - 1, -1)], axis=0)
-    token_ids = jnp.arange(tokens_here, dtype=jnp.int32)
-    same_row = token_ids[:, None] % QB == token_ids[None, :] % QB
-    home_blocks = position_ctx * blocks_here + token_ids // QB
-    home_targets = destination[home_blocks]
-
-    first_block = position_ctx * blocks_here
-    starts = lax.dynamic_slice_in_dim(doc_start, first_block, blocks_here, 0)
+    heads = lax.axis_size("head")
+    window, near = gather_kv(kv_rows, heads)
+    starts = lax.dynamic_slice_in_dim(doc_start, position_ctx * blocks_here, blocks_here, 0)
     base = (position_ctx * tokens_here).reshape(1)
-    flattened = attention(starts, base, queries, stacked[:, : 2 * DH], stacked[W1 - W2 :, 2 * DH :])
-    summed = summed_on_arrival(
-        lax.dot_general(
-            out_weight, flattened, (((0,), (1,)), ((), ())), preferred_element_type=jnp.float32
-        ),
-        "head",
-        0,
-    ).astype(jnp.bfloat16)
-    placed = jnp.zeros(summed.shape, jnp.float32)
-    for offset in range(-HOPS, HOPS + 1):
-        target_slots = (position_ctx + offset) * blocks_here + token_ids // QB
-        outgoing = jnp.dot(
-            summed,
-            ((home_targets[:, None] == target_slots[None, :]) & same_row).astype(jnp.bfloat16),
-            preferred_element_type=jnp.float32,
-        ).astype(jnp.bfloat16)
-        if offset != 0:
-            outgoing = passed_along(outgoing, "ctx", offset)
-        placed = placed + outgoing.astype(jnp.float32)
-    return placed.astype(jnp.bfloat16)
+    attended = attention(starts, base, queries, window, near)
+    return tail(destination, attended, out_weight, heads)
 
 
 def solution(mesh):

time: 123 us -> 76.7 us (0.62)
  the two profiles are of different devices: /device:TPU:96 before, /device:TPU:1 now
where the time goes in v2:
time: 76.7 us; the launch traced here: 76.5 us
  Pallas kernels  71.4 us (93%)
  local copies, waits for them, and re-layouts  5.07 us (7%)
    pallas_call x1, Pallas kernels, attention(): pl.pallas_call(attn_kernel, out_shape=jax.ShapeDtypeStruct((128, 512), jn...  26.8 us
    pallas_call x1, Pallas kernels, gather_kv(): pl.pallas_call(gather_kernel, out_shape=(jax.ShapeDtypeStruct((W1 + rows,...  25.8 us
    pallas_call x1, Pallas kernels, tail(): pl.pallas_call(tail_kernel, out_shape=jax.ShapeDtypeStruct((feats, tokens...  18.8 us
    unnamed x7, local copies, waits for them, and re-layouts  3.8 us

profile of v2, /device:TPU:1, one launch (start us, length us, event | category | flops | bytes accessed | tf_op | source)
XLA Modules:
  0.0 76.5 jit_solution(390208325326314982)
XLA Ops:
  0.0 1.3 %dynamic_slice.3.dstart_ref = s32[4]{0:T(128)} dynamic-slice(s32[256]{0:T(256)} %param.7, s32[]{:T(128)S(6)} %select_n.3), dynamic_slice_sizes={4} | dynamic-slice | bytes 36 | tf_op jit(solution)/shard_map/dynamic_slice | solution.py:221
  1.3 25.8 %shard_map.55 = (bf16[640,256]{1,0:T(8,128)(2,1)}, bf16[160,256]{1,0:T(8,128)(2,1)}) custom-call(bf16[128,512]{1,0:T(8,128)(2,1)} %kv_ref.1), custom_call_target="tpu_custom_call" | custom-call | tf_op jit(solution)/shard_map/pallas_call | solution.py:57
  27.1 26.8 %shard_map.56.att_ref = bf16[128,512]{1,0:T(8,128)(2,1)} custom-call(s32[4]{0:T(128)} %dynamic_slice.3.dstart_ref, s32[1]{0:T(128)} %bitcast.base_ref, bf16[128,512]{1,0:T(8,128)(2,1)} %q_ref.1, bf16[640,256]{1,0:T(8,128)(2,1)} %get-tuple-element.7.kvw_ref, bf16[160,256]{1,0:T(8,128)(2,1)} %get-tuple-element.8.near_ref), custom_call_target="tpu_custom_call" | custom-call | tf_op jit(solution)/shard_map/pallas_call | solution.py:205
  53.9 0.0 copy-start
  53.9 1.6 %copy-done = bf16[512,2048]{1,0:T(8,128)(2,1)S(1)} copy-done((bf16[512,2048]{1,0:T(8,128)(2,1)S(1)}, bf16[512,2048]{1,0:T(8,128)(2,1)}, u32[]{:S(2)}) %copy-start) | copy-done | bytes 2097176
  55.4 0.0 copy-start.1
  55.4 0.9 %copy-done.1 = bf16[128,512]{1,0:T(8,128)(2,1)S(1)} copy-done((bf16[128,512]{1,0:T(8,128)(2,1)S(1)}, bf16[128,512]{1,0:T(8,128)(2,1)}, u32[]{:S(2)}) %copy-start.1) | copy-done | bytes 131096
  56.4 0.0 copy-start.2
  56.4 0.7 copy-done.2
  57.0 18.8 %shard_map.57 = bf16[256,128]{1,0:T(8,128)(2,1)S(1)} custom-call(s32[256]{0:T(256)S(1)} %copy-done.2, bf16[128,512]{1,0:T(8,128)(2,1)S(1)} %copy-done.1, bf16[512,2048]{1,0:T(8,128)(2,1)S(1)} %copy-done), custom_call_target="tpu_custom_call" | custom-call | tf_op jit(solution)/shard_map/pallas_call | solution.py:120
  75.8 0.6 copy.7
Async XLA Ops:
  53.9 1.6 %copy-start = (bf16[512,2048]{1,0:T(8,128)(2,1)S(1)}, bf16[512,2048]{1,0:T(8,128)(2,1)}, u32[]{:S(2)}) copy-start(bf16[512,2048]{1,0:T(8,128)(2,1)} %w_ref.1) | copy-start | bytes 6291460
  55.4 0.9 %copy-start.1 = (bf16[128,512]{1,0:T(8,128)(2,1)S(1)}, bf16[128,512]{1,0:T(8,128)(2,1)}, u32[]{:S(2)}) copy-start(bf16[128,512]{1,0:T(8,128)(2,1)} %shard_map.56.att_ref) | copy-start | bytes 393220
  56.4 0.7 copy-start.2

commit v3 on v1

v3 whole, which is shorter than its diff:
```python
import jax
import jax.numpy as jnp
from jax import lax
from jax.experimental import pallas as pl
from jax.experimental.pallas import tpu as pltpu
from jax.sharding import PartitionSpec as P

DH = 128
W1 = 512
W2 = 32
QB = 32
GROUP = 4
BLOCKS = 4
HEADS_HERE = 4
ROWS = W1 + QB
UNIT = 4
STEPS = W2 // UNIT
UNROLL = 2
FAR_FIRST = (4, 3, 5, 2, 6, 7, 1)
CS = DH**-0.5 * 1.4426950408889634
BIG = -1e30


def remote(src, dst, send, recv, ctx, head):
    return pltpu.make_async_remote_copy(
        src_ref=src,
        dst_ref=dst,
        send_sem=send,
        recv_sem=recv,
        device_id=(ctx, head),
        device_id_type=pl.DeviceIdType.MESH,
    )


def prep_near(near, k2f, v2g, v2t):
    rows = near.shape[0]
    both = near[...].astype(jnp.float32)
    k2f[...] = both[:, :DH]
    v2t[:, :rows] = both[:, DH:].T
    v2t[:, rows:] = jnp.zeros((DH, v2t.shape[1] - rows), jnp.float32)
    lane = lax.broadcasted_iota(jnp.int32, (DH, DH), 1)
    full = v2t[...]
    for g in range(BLOCKS + 1):
        x = pltpu.roll(full, 2 * DH - (g * QB + 1), 1)[:, :DH]
        x = jnp.where(lane < QB, x, 0.0)
        x = x + pltpu.roll(x, QB, 1)
        v2g[g] = x + pltpu.roll(x, 2 * QB, 1)


def make_steps(starts, base, q_ref, k1x, v1t, k2f, v2g, acc):
    wide = UNIT * DH
    offset = lax.broadcasted_iota(jnp.int32, (QB, wide), 0)
    older = offset > lax.broadcasted_iota(jnp.int32, (QB, wide), 1) % QB
    lane = lax.broadcasted_iota(jnp.int32, (QB, DH), 1)
    tok = lax.broadcasted_iota(jnp.int32, (QB, DH), 0)
    lane_tok = lax.broadcasted_iota(jnp.int32, (DH, DH), 1) % QB

    def start_of(b):
        s = starts[0]
        for j in range(1, BLOCKS):
            s = jnp.where(b == j, starts[j], s)
        return s - base

    def scores(n, out):
        b = n // STEPS
        step = n % STEPS
        s = start_of(b)
        key_out = (lane < (W1 // QB + BLOCKS)) & (lane * QB - W1 < s)
        parts = []
        for u in range(UNIT):
            m = W2 - 1 - UNIT * step - u
            k2 = k2f[pl.ds(b * QB + m + 1, QB), :].astype(jnp.bfloat16)
            left_out = key_out | ((lane == QB) & (b * QB + tok + m - (W2 - 1) < s))
            bias = jnp.where(left_out, BIG, 0.0).astype(jnp.bfloat16)
            for h in range(HEADS_HERE):
                q = q_ref[pl.ds(pl.multiple_of(b * QB, QB), QB), h * DH : (h + 1) * DH]
                parts.append(jnp.concatenate([q * k2, bias], axis=1))
        rhs = jnp.concatenate(parts, axis=0)
        keys = k1x[pl.ds(pl.multiple_of(b * QB, QB), ROWS), :]
        r = lax.dot_general(
            keys, rhs, (((1,), (1,)), ((), ())), preferred_element_type=jnp.float32
        )
        out[:QB, :] = jnp.where(older, r[:QB], r[W1:])
        out[QB:, :] = r[QB:W1]

    def weigh(n, src, peak, total):
        b = n // STEPS
        step = n % STEPS
        s = src[...]
        column = s.max(axis=0, keepdims=True)
        new = peak
        for u in range(UNIT):
            new = jnp.maximum(new, column[:, u * DH : (u + 1) * DH])
        scale = jnp.exp2((peak - new) * CS)
        p = jnp.exp2((s - jnp.concatenate([new] * UNIT, axis=1)) * CS).astype(jnp.bfloat16)
        edge = p[:QB]
        zero = jnp.zeros_like(edge)
        p = jnp.concatenate(
            [jnp.where(older, edge, zero), p[QB:], jnp.where(older, zero, edge)], axis=0
        )
        o = jnp.dot(v1t[b], p, preferred_element_type=jnp.float32)
        total = total * scale
        a = acc[...] * scale
        for u in range(UNIT):
            m = W2 - 1 - UNIT * step - u
            total = total + o[DH : DH + 1, u * DH : (u + 1) * DH]
            v2 = pltpu.roll(jnp.where(lane_tok >= m, v2g[b], v2g[b + 1]), DH - m, 1)
            a = a + o[:DH, u * DH : (u + 1) * DH] * v2
        acc[...] = a
        return new, total

    return scores, weigh


def attend_block(b, scores, weigh, s0, s1, acc):
    acc[...] = jnp.zeros_like(acc)

    def pair(k, carry):
        n = b * STEPS + 2 * k
        scores(n + 1, s1)
        carry = weigh(n, s0, *carry)
        scores(jnp.minimum(n + 2, BLOCKS * STEPS - 1), s0)
        return weigh(n + 1, s1, *carry)

    first = (jnp.full((1, DH), BIG, jnp.float32), jnp.zeros((1, DH), jnp.float32))
    _, total = lax.fori_loop(0, STEPS // 2, pair, first, unroll=UNROLL)
    return (acc[...] / total).T.astype(jnp.bfloat16)


def kernel(
    start_ref, dest_ref, q_hbm, kv_hbm, w_hbm, out_ref,
    q_ref, kv_ref, w_ref, kvw, near, k1x, vt, v1t, k2f, v2g, v2t, s0, s1, acc,
    part, own, got, mine, grp,
    local_sem, send1, recv1, send2, recv2, near_sem, head_send, head_recv, group_send, group_recv,
):
    c = lax.axis_index("ctx")
    e = lax.axis_index("head")
    nc = lax.axis_size("ctx")
    nh = lax.axis_size("head")
    rows = kv_ref.shape[0]
    piece = rows // nh
    back = W1 // rows
    feats = out_ref.shape[0]
    place = lax.rem(c, GROUP)
    first_peer = c - place

    def head_peer(k):
        return lax.rem(e + k, nh)

    def group_peer(k):
        return first_peer + lax.rem(place + k, GROUP)

    loads = [
        pltpu.make_async_copy(kv_hbm, kv_ref, local_sem.at[0]),
        pltpu.make_async_copy(q_hbm, q_ref, local_sem.at[1]),
        pltpu.make_async_copy(w_hbm, w_ref, local_sem.at[2]),
    ]
    for load in loads:
        load.start()
    barrier = pltpu.get_barrier_semaphore()

    def greet(ctx, head):
        pl.semaphore_signal(
            barrier, inc=1, device_id=(ctx, head), device_id_type=pl.DeviceIdType.MESH
        )

    for d in range(back, 0, -1):
        greet(lax.rem(c + nc - d, nc), e)
    for k in range(1, nh):
        greet(c, head_peer(k))
    for k in range(1, GROUP):
        greet(group_peer(k), e)

    loads[0].wait()
    row = lax.broadcasted_iota(jnp.int32, (W1 + rows, DH), 0) // QB
    col = lax.broadcasted_iota(jnp.int32, (W1 + rows, DH), 1)
    k1x[:, DH:] = jnp.where((row == col) | (col == QB), 1.0, 0.0).astype(jnp.bfloat16)
    k1x[W1:, :DH] = kv_ref[:, :DH]
    near[W2:, :] = kv_ref[:, 2 * DH :]
    vt[:, W1:] = kv_ref[:, DH : 2 * DH].astype(jnp.float32).T
    for b in range(BLOCKS):
        v1t[b, DH:, :] = jnp.ones((16, ROWS), jnp.bfloat16)

    pl.semaphore_wait(barrier, back + nh - 1 + GROUP - 1)

    def slot(d, h):
        return kvw.at[pl.ds(pl.multiple_of((back - d) * rows + h * piece, piece), piece), :]

    mine_rows = kv_ref.at[pl.ds(pl.multiple_of(e * piece, piece), piece), pl.ds(0, 2 * DH)]
    first = {}
    for d in range(back, 0, -1):
        first[d] = remote(
            mine_rows, slot(d, e), send1.at[d - 1], recv1.at[d - 1], lax.rem(c + d, nc), e
        )
        first[d].start()
    last_rows = kv_ref.at[pl.ds(rows - W2, W2), pl.ds(2 * DH, 2 * DH)]
    beside = remote(
        last_rows, near.at[pl.ds(0, W2), :], near_sem.at[0], near_sem.at[1], lax.rem(c + 1, nc), e
    )
    beside.start()
    second = {}
    for d in range(1, back + 1):
        first[d].wait_recv()
        for k in range(1, nh):
            second[d, k] = remote(
                slot(d, e), slot(d, e), send2.at[d - 1, k - 1], recv2.at[d - 1, k - 1], c, head_peer(k)
            )
            second[d, k].start()
        if d == 1:
            beside.wait_recv()
            prep_near(near, k2f, v2g, v2t)
    for d in range(1, back + 1):
        for k in range(1, nh):
            second[d, k].wait_recv()
        at = (back - d) * rows
        k1x[at : at + rows, :DH] = kvw[at : at + rows, :DH]
        vt[:, at : at + rows] = kvw[at : at + rows, DH:].astype(jnp.float32).T
    for b in range(BLOCKS):
        v1t[b, :DH, :] = vt[:, b * QB : b * QB + ROWS].astype(jnp.bfloat16)

    starts = [start_ref[c * BLOCKS + j] for j in range(BLOCKS)]
    scores, weigh = make_steps(starts, c * rows, q_ref, k1x, v1t, k2f, v2g, acc)
    loads[1].wait()
    scores(0, s0)
    loads[2].wait()

    def to_head(b, k):
        return remote(
            part.at[b, k - 1], got.at[b, k - 1], head_send.at[b, k - 1], head_recv.at[b, k - 1],
            c, head_peer(k),
        )

    def to_group(b, k):
        return remote(
            mine.at[b], grp.at[k - 1, b], group_send.at[b, k - 1], group_recv.at[b, k - 1],
            group_peer(k), e,
        )

    def finish(b):
        total = own[b]
        for k in range(1, nh):
            to_head(b, k).wait_recv()
            total = total + got[b, k - 1].astype(jnp.float32)
        mine[b] = total.astype(jnp.bfloat16)
        for k in range(1, GROUP):
            to_group(b, k).start()

    def block(b, _):
        r = attend_block(b, scores, weigh, s0, s1, acc)
        a = jnp.concatenate([r[h * QB : (h + 1) * QB] for h in range(HEADS_HERE)], axis=1)

        def project(h):
            w = w_ref[:, pl.ds(pl.multiple_of(h * feats, feats), feats)]
            return jnp.dot(a, w, preferred_element_type=jnp.float32)

        for k in FAR_FIRST:
            if k < nh:
                part[b, k - 1] = project(head_peer(k)).astype(jnp.bfloat16)
                to_head(b, k).start()
        own[b] = project(e)

        @pl.when(b > 0)
        def _():
            finish(b - 1)

        return 0

    lax.fori_loop(0, BLOCKS, block, 0)
    finish(BLOCKS - 1)
    found = []
    for s in range(BLOCKS):
        where = jnp.int32(0)
        for j in range(GROUP * BLOCKS):
            where = jnp.where(dest_ref[first_peer * BLOCKS + j] == c * BLOCKS + s, j, where)
        found.append(where)
    for b in range(BLOCKS):
        for k in range(1, GROUP):
            to_group(b, k).wait_recv()
    picked = []
    for s in range(BLOCKS):
        source = lax.div(found[s], BLOCKS)
        b = lax.rem(found[s], BLOCKS)
        k = lax.rem(place - source + GROUP, GROUP)
        far = grp[jnp.maximum(k - 1, 0), b].astype(jnp.float32)
        here = mine[b].astype(jnp.float32)
        picked.append(jnp.where(k == 0, here, far))
    out_ref[...] = jnp.concatenate(picked, axis=0).T.astype(jnp.bfloat16)
    for d in range(1, back + 1):
        first[d].wait_send()
        for k in range(1, nh):
            second[d, k].wait_send()
    beside.wait_send()
    for b in range(BLOCKS):
        for k in range(1, nh):
            to_head(b, k).wait_send()
        for k in range(1, GROUP):
            to_group(b, k).wait_send()


def body(queries, kv_rows, doc_start, destination, out_weight):
    nh = lax.axis_size("head")
    rows = kv_rows.shape[0]
    back = W1 // rows
    feats = out_weight.shape[1] // nh
    half, full, dma = jnp.bfloat16, jnp.float32, pltpu.SemaphoreType.DMA
    smem = pl.BlockSpec(memory_space=pltpu.SMEM)
    anywhere = pl.BlockSpec(memory_space=pl.ANY)
    scratch = [
        pltpu.VMEM(queries.shape, half),
        pltpu.VMEM(kv_rows.shape, half),
        pltpu.VMEM(out_weight.shape, half),
        pltpu.VMEM((W1, 2 * DH), half),
        pltpu.VMEM((W2 + rows, 2 * DH), half),
        pltpu.VMEM((W1 + rows, 2 * DH), half),
        pltpu.VMEM((DH, W1 + rows), full),
        pltpu.VMEM((BLOCKS, DH + 16, ROWS), half),
        pltpu.VMEM((W2 + rows, DH), full),
        pltpu.VMEM((BLOCKS + 1, DH, DH), full),
        pltpu.VMEM((DH, 2 * DH), full),
        pltpu.VMEM((W1, UNIT * DH), full),
        pltpu.VMEM((W1, UNIT * DH), full),
        pltpu.VMEM((DH, DH), full),
        pltpu.VMEM((BLOCKS, nh - 1, QB, feats), half),
        pltpu.VMEM((BLOCKS, QB, feats), full),
        pltpu.VMEM((BLOCKS, nh - 1, QB, feats), half),
        pltpu.VMEM((BLOCKS, QB, feats), half),
        pltpu.VMEM((GROUP - 1, BLOCKS, QB, feats), half),
        dma((3,)),
        dma((back,)),
        dma((back,)),
        dma((back, nh - 1)),
        dma((back, nh - 1)),
        dma((2,)),
        dma((BLOCKS, nh - 1)),
        dma((BLOCKS, nh - 1)),
        dma((BLOCKS, GROUP - 1)),
        dma((BLOCKS, GROUP - 1)),
    ]
    return pl.pallas_call(
        kernel,
        out_shape=jax.ShapeDtypeStruct((feats, rows), half),
        in_specs=[smem, smem, anywhere, anywhere, anywhere],
        out_specs=pl.BlockSpec(memory_space=pltpu.VMEM),
        scratch_shapes=scratch,
        compiler_params=pltpu.CompilerParams(
            collective_id=0, has_side_effects=True, vmem_limit_bytes=60 * 2**20
        ),
    )(doc_start, destination, queries, kv_rows, out_weight)


def solution(mesh):
    in_specs = (P("ctx", "head"), P("ctx", None), P(), P(), P("head", None))
    out_specs = P("head", "ctx")
    return jax.shard_map(body, mesh=mesh, in_specs=in_specs, out_specs=out_specs, check_vma=False)
```

time: 123 us -> 54.4 us (0.44)
  the two profiles are of different devices: /device:TPU:96 before, /device:TPU:1 now
where the time goes in v3:
time: 54.4 us; the launch traced here: 54.2 us
  Pallas kernels  52.7 us (97%)
  local copies, waits for them, and re-layouts  1.47 us (3%)
    pallas_call x1, Pallas kernels, body(): pl.pallas_call(kernel, out_shape=jax.ShapeDtypeStruct((feats, rows), half...  52.7 us
    unnamed x1, local copies, waits for them, and re-layouts  1.47 us

profile of v3, /device:TPU:1, one launch (start us, length us, event | category | flops | bytes accessed | tf_op | source)
XLA Modules:
  0.0 54.2 jit_solution(9296375069075797851)
XLA Ops:
  0.0 52.7 %shard_map.55 = bf16[256,128]{1,0:T(8,128)(2,1)} custom-call(s32[256]{0:T(256)} %start_ref.1, s32[256]{0:T(256)} %dest_ref.1, bf16[128,512]{1,0:T(8,128)(2,1)} %q_hbm.1, bf16[128,512]{1,0:T(8,128)(2,1)} %kv_hbm.1, bf16[512,2048]{1,0:T(8,128)(2,1)} %w_hbm.1), custom_call_target="tpu_custom_call" | custom-call | tf_op jit(solution)/shard_map/pallas_call | solution.py:339
  52.7 1.5 %copy.7 = bf16[256,128]{1,0:T(8,128)(2,1)} copy(bf16[256,128]{1,0:T(8,128)(2,1)} %shard_map.55) | data formatting | bytes 131072

commit v4 on v3

--- a/solution.py
+++ b/solution.py
@@ -15,7 +15,7 @@
 ROWS = W1 + QB
 UNIT = 4
 STEPS = W2 // UNIT
-UNROLL = 2
+UNROLL = 4
 FAR_FIRST = (4, 3, 5, 2, 6, 7, 1)
 CS = DH**-0.5 * 1.4426950408889634
 BIG = -1e30
@@ -117,10 +117,11 @@
 
     def pair(k, carry):
         n = b * STEPS + 2 * k
-        scores(n + 1, s1)
         carry = weigh(n, s0, *carry)
         scores(jnp.minimum(n + 2, BLOCKS * STEPS - 1), s0)
-        return weigh(n + 1, s1, *carry)
+        carry = weigh(n + 1, s1, *carry)
+        scores(jnp.minimum(n + 3, BLOCKS * STEPS - 1), s1)
+        return carry
 
     first = (jnp.full((1, DH), BIG, jnp.float32), jnp.zeros((1, DH), jnp.float32))
     _, total = lax.fori_loop(0, STEPS // 2, pair, first, unroll=UNROLL)
@@ -140,7 +141,7 @@
     rows = kv_ref.shape[0]
     piece = rows // nh
     back = W1 // rows
-    feats = out_ref.shape[0]
+    feats = out_ref.shape[1]
     place = lax.rem(c, GROUP)
     first_peer = c - place
 
@@ -222,6 +223,7 @@
     scores, weigh = make_steps(starts, c * rows, q_ref, k1x, v1t, k2f, v2g, acc)
     loads[1].wait()
     scores(0, s0)
+    scores(1, s1)
     loads[2].wait()
 
     def to_head(b, k):
@@ -284,7 +286,7 @@
         far = grp[jnp.maximum(k - 1, 0), b].astype(jnp.float32)
         here = mine[b].astype(jnp.float32)
         picked.append(jnp.where(k == 0, here, far))
-    out_ref[...] = jnp.concatenate(picked, axis=0).T.astype(jnp.bfloat16)
+    out_ref[...] = jnp.concatenate(picked, axis=0).astype(jnp.bfloat16)
     for d in range(1, back + 1):
         first[d].wait_send()
         for k in range(1, nh):
@@ -336,9 +338,9 @@
         dma((BLOCKS, GROUP - 1)),
         dma((BLOCKS, GROUP - 1)),
     ]
-    return pl.pallas_call(
+    stored = pl.pallas_call(
         kernel,
-        out_shape=jax.ShapeDtypeStruct((feats, rows), half),
+        out_shape=jax.ShapeDtypeStruct((rows, feats), half),
         in_specs=[smem, smem, anywhere, anywhere, anywhere],
         out_specs=pl.BlockSpec(memory_space=pltpu.VMEM),
         scratch_shapes=scratch,
@@ -346,6 +348,7 @@
             collective_id=0, has_side_effects=True, vmem_limit_bytes=60 * 2**20
         ),
     )(doc_start, destination, queries, kv_rows, out_weight)
+    return stored.T
 
 
 def solution(mesh):

time: 54.4 us -> 52.1 us (0.958)
  Pallas kernels: 52.7 us -> 50.3 us
    pallas_call x1, Pallas kernels: 52.7 us -> 50.3 us  [body(): pl.pallas_call(kernel, out_shape=jax.ShapeDtypeStruct((rows, feats), half...]
    transpose x0 -> x1, local copies, waits for them, and re-layouts: none -> 1.57 us  [body(): return stored.T]
    unnamed x1 -> x0, local copies, waits for them, and re-layouts: 1.47 us -> none
where the time goes in v4:
time: 52.1 us; the launch traced here: 51.9 us
  Pallas kernels  50.3 us (97%)
  local copies, waits for them, and re-layouts  1.57 us (3%)
    pallas_call x1, Pallas kernels, body(): pl.pallas_call(kernel, out_shape=jax.ShapeDtypeStruct((rows, feats), half...  50.3 us
    transpose x1, local copies, waits for them, and re-layouts, body(): return stored.T  1.57 us

profile of v4, /device:TPU:1, one launch (start us, length us, event | category | flops | bytes accessed | tf_op | source)
XLA Modules:
  0.0 51.9 jit_solution(10573389001418381702)
XLA Ops:
  0.0 50.3 %shard_map.55 = bf16[128,256]{1,0:T(8,128)(2,1)} custom-call(s32[256]{0:T(256)} %start_ref.1, s32[256]{0:T(256)} %dest_ref.1, bf16[128,512]{1,0:T(8,128)(2,1)} %q_hbm.1, bf16[128,512]{1,0:T(8,128)(2,1)} %kv_hbm.1, bf16[512,2048]{1,0:T(8,128)(2,1)} %w_hbm.1), custom_call_target="tpu_custom_call" | custom-call | tf_op jit(solution)/shard_map/pallas_call | solution.py:341
  50.3 1.6 %copy.6 = bf16[256,128]{1,0:T(8,128)(2,1)} copy(bf16[256,128]{0,1:T(8,128)(2,1)} %bitcast.1) | data formatting | bytes 131072 | tf_op jit(solution)/shard_map/transpose | solution.py:351

commit v5 on v4

--- a/solution.py
+++ b/solution.py
@@ -12,7 +12,8 @@
 GROUP = 4
 BLOCKS = 4
 HEADS_HERE = 4
-ROWS = W1 + QB
+NEAR = W1 // 2 + QB
+FAR = W1 // 2
 UNIT = 4
 STEPS = W2 // UNIT
 UNROLL = 4
@@ -47,10 +48,11 @@
         v2g[g] = x + pltpu.roll(x, 2 * QB, 1)
 
 
-def make_steps(starts, base, q_ref, k1x, v1t, k2f, v2g, acc):
+def make_steps(starts, base, q_ref, k1x, values, k2f, v2g, acc, first_row, count, edge):
     wide = UNIT * DH
     offset = lax.broadcasted_iota(jnp.int32, (QB, wide), 0)
     older = offset > lax.broadcasted_iota(jnp.int32, (QB, wide), 1) % QB
+    edge_in = older if edge == 0 else jnp.logical_not(older)
     lane = lax.broadcasted_iota(jnp.int32, (QB, DH), 1)
     tok = lax.broadcasted_iota(jnp.int32, (QB, DH), 0)
     lane_tok = lax.broadcasted_iota(jnp.int32, (DH, DH), 1) % QB
@@ -76,12 +78,16 @@
                 q = q_ref[pl.ds(pl.multiple_of(b * QB, QB), QB), h * DH : (h + 1) * DH]
                 parts.append(jnp.concatenate([q * k2, bias], axis=1))
         rhs = jnp.concatenate(parts, axis=0)
-        keys = k1x[pl.ds(pl.multiple_of(b * QB, QB), ROWS), :]
+        keys = k1x[pl.ds(pl.multiple_of(b * QB + first_row, QB), count), :]
         r = lax.dot_general(
             keys, rhs, (((1,), (1,)), ((), ())), preferred_element_type=jnp.float32
         )
-        out[:QB, :] = jnp.where(older, r[:QB], r[W1:])
-        out[QB:, :] = r[QB:W1]
+        end = edge + QB
+        if edge:
+            out[:edge, :] = r[:edge]
+        out[edge:end, :] = jnp.where(edge_in, r[edge:end], BIG)
+        if end < count:
+            out[end:, :] = r[end:]
 
     def weigh(n, src, peak, total):
         b = n // STEPS
@@ -93,28 +99,21 @@
             new = jnp.maximum(new, column[:, u * DH : (u + 1) * DH])
         scale = jnp.exp2((peak - new) * CS)
         p = jnp.exp2((s - jnp.concatenate([new] * UNIT, axis=1)) * CS).astype(jnp.bfloat16)
-        edge = p[:QB]
-        zero = jnp.zeros_like(edge)
-        p = jnp.concatenate(
-            [jnp.where(older, edge, zero), p[QB:], jnp.where(older, zero, edge)], axis=0
-        )
-        o = jnp.dot(v1t[b], p, preferred_element_type=jnp.float32)
+        o = jnp.dot(values[b], p, preferred_element_type=jnp.float32)
         total = total * scale
-        a = acc[...] * scale
+        a = acc[b] * scale
         for u in range(UNIT):
             m = W2 - 1 - UNIT * step - u
             total = total + o[DH : DH + 1, u * DH : (u + 1) * DH]
             v2 = pltpu.roll(jnp.where(lane_tok >= m, v2g[b], v2g[b + 1]), DH - m, 1)
             a = a + o[:DH, u * DH : (u + 1) * DH] * v2
-        acc[...] = a
+        acc[b] = a
         return new, total
 
     return scores, weigh
 
 
-def attend_block(b, scores, weigh, s0, s1, acc):
-    acc[...] = jnp.zeros_like(acc)
-
+def attend_block(b, scores, weigh, s0, s1, first):
     def pair(k, carry):
         n = b * STEPS + 2 * k
         carry = weigh(n, s0, *carry)
@@ -123,14 +122,12 @@
         scores(jnp.minimum(n + 3, BLOCKS * STEPS - 1), s1)
         return carry
 
-    first = (jnp.full((1, DH), BIG, jnp.float32), jnp.zeros((1, DH), jnp.float32))
-    _, total = lax.fori_loop(0, STEPS // 2, pair, first, unroll=UNROLL)
-    return (acc[...] / total).T.astype(jnp.bfloat16)
+    return lax.fori_loop(0, STEPS // 2, pair, first, unroll=UNROLL)
 
 
 def kernel(
     start_ref, dest_ref, q_hbm, kv_hbm, w_hbm, out_ref,
-    q_ref, kv_ref, w_ref, kvw, near, k1x, vt, v1t, k2f, v2g, v2t, s0, s1, acc,
+    q_ref, kv_ref, w_ref, kvw, near, k1x, vt, v1n, v1f, k2f, v2g, v2t, n0, n1, f0, f1, acc, state,
     part, own, got, mine, grp,
     local_sem, send1, recv1, send2, recv2, near_sem, head_send, head_recv, group_send, group_recv,
 ):
@@ -180,7 +177,8 @@
     near[W2:, :] = kv_ref[:, 2 * DH :]
     vt[:, W1:] = kv_ref[:, DH : 2 * DH].astype(jnp.float32).T
     for b in range(BLOCKS):
-        v1t[b, DH:, :] = jnp.ones((16, ROWS), jnp.bfloat16)
+        v1n[b, DH:, :] = jnp.ones((16, NEAR), jnp.bfloat16)
+        v1f[b, DH:, :] = jnp.ones((16, FAR), jnp.bfloat16)
 
     pl.semaphore_wait(barrier, back + nh - 1 + GROUP - 1)
 
@@ -199,31 +197,65 @@
         last_rows, near.at[pl.ds(0, W2), :], near_sem.at[0], near_sem.at[1], lax.rem(c + 1, nc), e
     )
     beside.start()
+    half_back = back // 2
     second = {}
-    for d in range(1, back + 1):
+
+    def spread(d):
         first[d].wait_recv()
         for k in range(1, nh):
-            second[d, k] = remote(
-                slot(d, e), slot(d, e), send2.at[d - 1, k - 1], recv2.at[d - 1, k - 1], c, head_peer(k)
-            )
             second[d, k].start()
-        if d == 1:
-            beside.wait_recv()
-            prep_near(near, k2f, v2g, v2t)
-    for d in range(1, back + 1):
+
+    def take(d):
         for k in range(1, nh):
             second[d, k].wait_recv()
         at = (back - d) * rows
         k1x[at : at + rows, :DH] = kvw[at : at + rows, :DH]
         vt[:, at : at + rows] = kvw[at : at + rows, DH:].astype(jnp.float32).T
-    for b in range(BLOCKS):
-        v1t[b, :DH, :] = vt[:, b * QB : b * QB + ROWS].astype(jnp.bfloat16)
+
+    for d in range(1, back + 1):
+        for k in range(1, nh):
+            second[d, k] = remote(
+                slot(d, e), slot(d, e), send2.at[d - 1, k - 1], recv2.at[d - 1, k - 1], c, head_peer(k)
+            )
+    for d in range(1, half_back + 1):
+        spread(d)
+    beside.wait_recv()
+    prep_near(near, k2f, v2g, v2t)
+    for d in range(1, half_back + 1):
+        take(d)
+    for b in range(BLOCKS):
+        at = b * QB + FAR
+        v1n[b, :DH, :] = vt[:, at : at + NEAR].astype(jnp.bfloat16)
 
     starts = [start_ref[c * BLOCKS + j] for j in range(BLOCKS)]
-    scores, weigh = make_steps(starts, c * rows, q_ref, k1x, v1t, k2f, v2g, acc)
+    shared = (starts, c * rows, q_ref, k1x)
+    near_scores, near_weigh = make_steps(*shared, v1n, k2f, v2g, acc, FAR, NEAR, NEAR - QB)
+    far_scores, far_weigh = make_steps(*shared, v1f, k2f, v2g, acc, 0, FAR, 0)
     loads[1].wait()
-    scores(0, s0)
-    scores(1, s1)
+    near_scores(0, n0)
+    near_scores(1, n1)
+
+    def near_block(b, _):
+        acc[b] = jnp.zeros((DH, DH), jnp.float32)
+        nothing = (jnp.full((1, DH), BIG, jnp.float32), jnp.zeros((1, DH), jnp.float32))
+        peak, total = attend_block(b, near_scores, near_weigh, n0, n1, nothing)
+        state[b, 0:1, :] = peak
+        state[b, 1:2, :] = total
+
+        @pl.when(b == 0)
+        def _():
+            for d in range(half_back + 1, back + 1):
+                spread(d)
+
+        return 0
+
+    lax.fori_loop(0, BLOCKS, near_block, 0)
+    for d in range(half_back + 1, back + 1):
+        take(d)
+    for b in range(BLOCKS):
+        v1f[b, :DH, :] = vt[:, b * QB : b * QB + FAR].astype(jnp.bfloat16)
+    far_scores(0, f0)
+    far_scores(1, f1)
     loads[2].wait()
 
     def to_head(b, k):
@@ -248,7 +280,9 @@
             to_group(b, k).start()
 
     def block(b, _):
-        r = attend_block(b, scores, weigh, s0, s1, acc)
+        carry = (state[b, 0:1, :], state[b, 1:2, :])
+        _, total = attend_block(b, far_scores, far_weigh, f0, f1, carry)
+        r = (acc[b] / total).T.astype(jnp.bfloat16)
         a = jnp.concatenate([r[h * QB : (h + 1) * QB] for h in range(HEADS_HERE)], axis=1)
 
         def project(h):
@@ -315,13 +349,17 @@
         pltpu.VMEM((W2 + rows, 2 * DH), half),
         pltpu.VMEM((W1 + rows, 2 * DH), half),
         pltpu.VMEM((DH, W1 + rows), full),
-        pltpu.VMEM((BLOCKS, DH + 16, ROWS), half),
+        pltpu.VMEM((BLOCKS, DH + 16, NEAR), half),
+        pltpu.VMEM((BLOCKS, DH + 16, FAR), half),
         pltpu.VMEM((W2 + rows, DH), full),
         pltpu.VMEM((BLOCKS + 1, DH, DH), full),
         pltpu.VMEM((DH, 2 * DH), full),
-        pltpu.VMEM((W1, UNIT * DH), full),
-        pltpu.VMEM((W1, UNIT * DH), full),
-        pltpu.VMEM((DH, DH), full),
+        pltpu.VMEM((NEAR, UNIT * DH), full),
+        pltpu.VMEM((NEAR, UNIT * DH), full),
+        pltpu.VMEM((FAR, UNIT * DH), full),
+        pltpu.VMEM((FAR, UNIT * DH), full),
+        pltpu.VMEM((BLOCKS, DH, DH), full),
+        pltpu.VMEM((BLOCKS, 8, DH), full),
         pltpu.VMEM((BLOCKS, nh - 1, QB, feats), half),
         pltpu.VMEM((BLOCKS, QB, feats), full),
         pltpu.VMEM((BLOCKS, nh - 1, QB, feats), half),

time: 52.1 us -> 55.6 us (1.067)
  Pallas kernels: 50.3 us -> 53.8 us
    pallas_call x1, Pallas kernels: 50.3 us -> 53.8 us  [body(): pl.pallas_call(kernel, out_shape=jax.ShapeDtypeStruct((rows, feats), half...]
where the time goes in v5:
time: 55.6 us; the launch traced here: 55.4 us
  Pallas kernels  53.8 us (97%)
  local copies, waits for them, and re-layouts  1.57 us (3%)
    pallas_call x1, Pallas kernels, body(): pl.pallas_call(kernel, out_shape=jax.ShapeDtypeStruct((rows, feats), half...  53.8 us
    transpose x1, local copies, waits for them, and re-layouts, body(): return stored.T  1.57 us

profile of v5, /device:TPU:1, one launch (start us, length us, event | category | flops | bytes accessed | tf_op | source)
XLA Modules:
  0.0 55.4 jit_solution(1517692813419374521)
XLA Ops:
  0.0 53.8 %shard_map.55 = bf16[128,256]{1,0:T(8,128)(2,1)} custom-call(s32[256]{0:T(256)} %start_ref.1, s32[256]{0:T(256)} %dest_ref.1, bf16[128,512]{1,0:T(8,128)(2,1)} %q_hbm.1, bf16[128,512]{1,0:T(8,128)(2,1)} %kv_hbm.1, bf16[512,2048]{1,0:T(8,128)(2,1)} %w_hbm.1), custom_call_target="tpu_custom_call" | custom-call | tf_op jit(solution)/shard_map/pallas_call | solution.py:379
  53.8 1.6 %copy.6 = bf16[256,128]{1,0:T(8,128)(2,1)} copy(bf16[256,128]{0,1:T(8,128)(2,1)} %bitcast.1) | data formatting | bytes 131072 | tf_op jit(solution)/shard_map/transpose | solution.py:389

commit v6 on v4

--- a/solution.py
+++ b/solution.py
@@ -32,7 +32,25 @@
     )
 
 
-def prep_near(near, k2f, v2g, v2t):
+def prep_bias(starts, base, k2x):
+    tok = lax.broadcasted_iota(jnp.int32, (BLOCKS * QB, DH), 0)
+    lane = lax.broadcasted_iota(jnp.int32, (BLOCKS * QB, DH), 1)
+    s = starts[0]
+    for j in range(1, BLOCKS):
+        s = jnp.where(tok < j * QB, s, starts[j])
+    s = s - base
+    key_out = (lane < (W1 // QB + BLOCKS)) & (lane * QB - W1 < s)
+    reach = jnp.where(lane == QB, s - tok + (W2 - 1), 0)
+    fixed = jnp.where(key_out, BIG, 0.0)
+
+    def one(m, _):
+        k2x[m, :, DH:] = jnp.where(m < reach, BIG, fixed).astype(jnp.bfloat16)
+        return 0
+
+    lax.fori_loop(0, W2, one, 0, unroll=4)
+
+
+def prep_near(near, k2f, k2x, v2g, v2t, v2x):
     rows = near.shape[0]
     both = near[...].astype(jnp.float32)
     k2f[...] = both[:, :DH]
@@ -45,35 +63,34 @@
         x = jnp.where(lane < QB, x, 0.0)
         x = x + pltpu.roll(x, QB, 1)
         v2g[g] = x + pltpu.roll(x, 2 * QB, 1)
-
-
-def make_steps(starts, base, q_ref, k1x, v1t, k2f, v2g, acc):
+    for m in range(W2):
+        k2x[m, :, :DH] = k2f[m + 1 : m + 1 + BLOCKS * QB, :].astype(jnp.bfloat16)
+
+    def one(m, _):
+        for b in range(BLOCKS):
+            x = jnp.where(lane % QB >= m, v2g[b], v2g[b + 1])
+            v2x[m, b] = pltpu.roll(x, DH - m, 1)
+        return 0
+
+    lax.fori_loop(0, W2, one, 0)
+
+
+def make_steps(q_ref, k1x, v1t, k2x, v2x, acc):
     wide = UNIT * DH
     offset = lax.broadcasted_iota(jnp.int32, (QB, wide), 0)
     older = offset > lax.broadcasted_iota(jnp.int32, (QB, wide), 1) % QB
-    lane = lax.broadcasted_iota(jnp.int32, (QB, DH), 1)
-    tok = lax.broadcasted_iota(jnp.int32, (QB, DH), 0)
-    lane_tok = lax.broadcasted_iota(jnp.int32, (DH, DH), 1) % QB
-
-    def start_of(b):
-        s = starts[0]
-        for j in range(1, BLOCKS):
-            s = jnp.where(b == j, starts[j], s)
-        return s - base
 
     def scores(n, out):
         b = n // STEPS
         step = n % STEPS
-        s = start_of(b)
-        key_out = (lane < (W1 // QB + BLOCKS)) & (lane * QB - W1 < s)
+        here = pl.ds(pl.multiple_of(b * QB, QB), QB)
         parts = []
         for u in range(UNIT):
             m = W2 - 1 - UNIT * step - u
-            k2 = k2f[pl.ds(b * QB + m + 1, QB), :].astype(jnp.bfloat16)
-            left_out = key_out | ((lane == QB) & (b * QB + tok + m - (W2 - 1) < s))
-            bias = jnp.where(left_out, BIG, 0.0).astype(jnp.bfloat16)
+            k2 = k2x[m, here, :DH]
+            bias = k2x[m, here, DH:]
             for h in range(HEADS_HERE):
-                q = q_ref[pl.ds(pl.multiple_of(b * QB, QB), QB), h * DH : (h + 1) * DH]
+                q = q_ref[here, h * DH : (h + 1) * DH]
                 parts.append(jnp.concatenate([q * k2, bias], axis=1))
         rhs = jnp.concatenate(parts, axis=0)
         keys = k1x[pl.ds(pl.multiple_of(b * QB, QB), ROWS), :]
@@ -104,8 +121,7 @@
         for u in range(UNIT):
             m = W2 - 1 - UNIT * step - u
             total = total + o[DH : DH + 1, u * DH : (u + 1) * DH]
-            v2 = pltpu.roll(jnp.where(lane_tok >= m, v2g[b], v2g[b + 1]), DH - m, 1)
-            a = a + o[:DH, u * DH : (u + 1) * DH] * v2
+            a = a + o[:DH, u * DH : (u + 1) * DH] * v2x[m, b]
         acc[...] = a
         return new, total
 
@@ -130,8 +146,8 @@
 
 def kernel(
     start_ref, dest_ref, q_hbm, kv_hbm, w_hbm, out_ref,
-    q_ref, kv_ref, w_ref, kvw, near, k1x, vt, v1t, k2f, v2g, v2t, s0, s1, acc,
-    part, own, got, mine, grp,
+    q_ref, kv_ref, w_ref, kvw, near, k1x, vt, v1t, k2f, k2x, v2g, v2t, v2x, s0, s1, acc,
+    product, part, own, got, mine, grp,
     local_sem, send1, recv1, send2, recv2, near_sem, head_send, head_recv, group_send, group_recv,
 ):
     c = lax.axis_index("ctx")
@@ -173,6 +189,23 @@
         greet(group_peer(k), e)
 
     loads[0].wait()
+    pl.semaphore_wait(barrier, back + nh - 1 + GROUP - 1)
+
+    def slot(d, h):
+        return kvw.at[pl.ds(pl.multiple_of((back - d) * rows + h * piece, piece), piece), :]
+
+    mine_rows = kv_ref.at[pl.ds(pl.multiple_of(e * piece, piece), piece), pl.ds(0, 2 * DH)]
+    first = {}
+    for d in range(back, 0, -1):
+        first[d] = remote(
+            mine_rows, slot(d, e), send1.at[d - 1], recv1.at[d - 1], lax.rem(c + d, nc), e
+        )
+        first[d].start()
+    last_rows = kv_ref.at[pl.ds(rows - W2, W2), pl.ds(2 * DH, 2 * DH)]
+    beside = remote(
+        last_rows, near.at[pl.ds(0, W2), :], near_sem.at[0], near_sem.at[1], lax.rem(c + 1, nc), e
+    )
+    beside.start()
     row = lax.broadcasted_iota(jnp.int32, (W1 + rows, DH), 0) // QB
     col = lax.broadcasted_iota(jnp.int32, (W1 + rows, DH), 1)
     k1x[:, DH:] = jnp.where((row == col) | (col == QB), 1.0, 0.0).astype(jnp.bfloat16)
@@ -182,23 +215,8 @@
     for b in range(BLOCKS):
         v1t[b, DH:, :] = jnp.ones((16, ROWS), jnp.bfloat16)
 
-    pl.semaphore_wait(barrier, back + nh - 1 + GROUP - 1)
-
-    def slot(d, h):
-        return kvw.at[pl.ds(pl.multiple_of((back - d) * rows + h * piece, piece), piece), :]
-
-    mine_rows = kv_ref.at[pl.ds(pl.multiple_of(e * piece, piece), piece), pl.ds(0, 2 * DH)]
-    first = {}
-    for d in range(back, 0, -1):
-        first[d] = remote(
-            mine_rows, slot(d, e), send1.at[d - 1], recv1.at[d - 1], lax.rem(c + d, nc), e
-        )
-        first[d].start()
-    last_rows = kv_ref.at[pl.ds(rows - W2, W2), pl.ds(2 * DH, 2 * DH)]
-    beside = remote(
-        last_rows, near.at[pl.ds(0, W2), :], near_sem.at[0], near_sem.at[1], lax.rem(c + 1, nc), e
-    )
-    beside.start()
+    starts = [start_ref[c * BLOCKS + j] for j in range(BLOCKS)]
+    prep_bias(starts, c * rows, k2x)
     second = {}
     for d in range(1, back + 1):
         first[d].wait_recv()
@@ -207,9 +225,10 @@
                 slot(d, e), slot(d, e), send2.at[d - 1, k - 1], recv2.at[d - 1, k - 1], c, head_peer(k)
             )
             second[d, k].start()
-        if d == 1:
-            beside.wait_recv()
-            prep_near(near, k2f, v2g, v2t)
+    beside.wait_recv()
+    prep_near(near, k2f, k2x, v2g, v2t, v2x)
+    loads[1].wait()
+    loads[2].wait()
     for d in range(1, back + 1):
         for k in range(1, nh):
             second[d, k].wait_recv()
@@ -219,17 +238,17 @@
     for b in range(BLOCKS):
         v1t[b, :DH, :] = vt[:, b * QB : b * QB + ROWS].astype(jnp.bfloat16)
 
-    starts = [start_ref[c * BLOCKS + j] for j in range(BLOCKS)]
-    scores, weigh = make_steps(starts, c * rows, q_ref, k1x, v1t, k2f, v2g, acc)
-    loads[1].wait()
+    scores, weigh = make_steps(q_ref, k1x, v1t, k2x, v2x, acc)
     scores(0, s0)
     scores(1, s1)
-    loads[2].wait()
+
+    def columns_of(h):
+        return pl.ds(pl.multiple_of(h * feats, feats), feats)
 
     def to_head(b, k):
         return remote(
-            part.at[b, k - 1], got.at[b, k - 1], head_send.at[b, k - 1], head_recv.at[b, k - 1],
-            c, head_peer(k),
+            part.at[b, :, columns_of(head_peer(k))], got.at[b, k - 1],
+            head_send.at[b, k - 1], head_recv.at[b, k - 1], c, head_peer(k),
         )
 
     def to_group(b, k):
@@ -251,15 +270,12 @@
         r = attend_block(b, scores, weigh, s0, s1, acc)
         a = jnp.concatenate([r[h * QB : (h + 1) * QB] for h in range(HEADS_HERE)], axis=1)
 
-        def project(h):
-            w = w_ref[:, pl.ds(pl.multiple_of(h * feats, feats), feats)]
-            return jnp.dot(a, w, preferred_element_type=jnp.float32)
-
+        product[...] = jnp.dot(a, w_ref[...], preferred_element_type=jnp.float32)
+        part[b] = product[...].astype(jnp.bfloat16)
         for k in FAR_FIRST:
             if k < nh:
-                part[b, k - 1] = project(head_peer(k)).astype(jnp.bfloat16)
                 to_head(b, k).start()
-        own[b] = project(e)
+        own[b] = product[:, columns_of(e)]
 
         @pl.when(b > 0)
         def _():
@@ -268,7 +284,15 @@
         return 0
 
     lax.fori_loop(0, BLOCKS, block, 0)
+    for d in range(1, back + 1):
+        first[d].wait_send()
+        for k in range(1, nh):
+            second[d, k].wait_send()
+    beside.wait_send()
     finish(BLOCKS - 1)
+    for b in range(BLOCKS):
+        for k in range(1, nh):
+            to_head(b, k).wait_send()
     found = []
     for s in range(BLOCKS):
         where = jnp.int32(0)
@@ -287,14 +311,7 @@
         here = mine[b].astype(jnp.float32)
         picked.append(jnp.where(k == 0, here, far))
     out_ref[...] = jnp.concatenate(picked, axis=0).astype(jnp.bfloat16)
-    for d in range(1, back + 1):
-        first[d].wait_send()
-        for k in range(1, nh):
-            second[d, k].wait_send()
-    beside.wait_send()
-    for b in range(BLOCKS):
-        for k in range(1, nh):
-            to_head(b, k).wait_send()
+    for b in range(BLOCKS):
         for k in range(1, GROUP):
             to_group(b, k).wait_send()
 
@@ -317,12 +334,15 @@
         pltpu.VMEM((DH, W1 + rows), full),
         pltpu.VMEM((BLOCKS, DH + 16, ROWS), half),
         pltpu.VMEM((W2 + rows, DH), full),
+        pltpu.VMEM((W2, rows, 2 * DH), half),
         pltpu.VMEM((BLOCKS + 1, DH, DH), full),
         pltpu.VMEM((DH, 2 * DH), full),
+        pltpu.VMEM((W2, BLOCKS, DH, DH), full),
         pltpu.VMEM((W1, UNIT * DH), full),
         pltpu.VMEM((W1, UNIT * DH), full),
         pltpu.VMEM((DH, DH), full),
-        pltpu.VMEM((BLOCKS, nh - 1, QB, feats), half),
+        pltpu.VMEM((QB, nh * feats), full),
+        pltpu.VMEM((BLOCKS, QB, nh * feats), half),
         pltpu.VMEM((BLOCKS, QB, feats), full),
         pltpu.VMEM((BLOCKS, nh - 1, QB, feats), half),
         pltpu.VMEM((BLOCKS, QB, feats), half),

time: 52.1 us -> 50.4 us (0.967)
  Pallas kernels: 50.3 us -> 48.7 us
    pallas_call x1, Pallas kernels: 50.3 us -> 48.7 us  [body(): pl.pallas_call(kernel, out_shape=jax.ShapeDtypeStruct((rows, feats), half...]
where the time goes in v6:
time: 50.4 us; the launch traced here: 50.3 us
  Pallas kernels  48.7 us (97%)
  local copies, waits for them, and re-layouts  1.57 us (3%)
    pallas_call x1, Pallas kernels, body(): pl.pallas_call(kernel, out_shape=jax.ShapeDtypeStruct((rows, feats), half...  48.7 us
    transpose x1, local copies, waits for them, and re-layouts, body(): return stored.T  1.57 us

profile of v6, /device:TPU:1, one launch (start us, length us, event | category | flops | bytes accessed | tf_op | source)
XLA Modules:
  0.0 50.3 jit_solution(16790334008530804284)
XLA Ops:
  0.0 48.7 %shard_map.55 = bf16[128,256]{1,0:T(8,128)(2,1)} custom-call(s32[256]{0:T(256)} %start_ref.1, s32[256]{0:T(256)} %dest_ref.1, bf16[128,512]{1,0:T(8,128)(2,1)} %q_hbm.1, bf16[128,512]{1,0:T(8,128)(2,1)} %kv_hbm.1, bf16[512,2048]{1,0:T(8,128)(2,1)} %w_hbm.1), custom_call_target="tpu_custom_call" | custom-call | tf_op jit(solution)/shard_map/pallas_call | solution.py:361
  48.7 1.6 %copy.6 = bf16[256,128]{1,0:T(8,128)(2,1)} copy(bf16[256,128]{0,1:T(8,128)(2,1)} %bitcast.1) | data formatting | bytes 131072 | tf_op jit(solution)/shard_map/transpose | solution.py:371

commit v7 on v6

--- a/solution.py
+++ b/solution.py
@@ -13,9 +13,9 @@
 BLOCKS = 4
 HEADS_HERE = 4
 ROWS = W1 + QB
-UNIT = 4
+UNIT = 8
 STEPS = W2 // UNIT
-UNROLL = 4
+UNROLL = 2
 FAR_FIRST = (4, 3, 5, 2, 6, 7, 1)
 CS = DH**-0.5 * 1.4426950408889634
 BIG = -1e30
@@ -97,14 +97,19 @@
         r = lax.dot_general(
             keys, rhs, (((1,), (1,)), ((), ())), preferred_element_type=jnp.float32
         )
-        out[:QB, :] = jnp.where(older, r[:QB], r[W1:])
-        out[QB:, :] = r[QB:W1]
+        edge = jnp.where(older, r[:QB], r[W1:])
+        body_rows = r[QB:W1]
+        out[:QB, :] = edge
+        out[QB:W1, :] = body_rows
+        out[W1 : W1 + 1, :] = jnp.maximum(
+            edge.max(axis=0, keepdims=True), body_rows.max(axis=0, keepdims=True)
+        )
 
     def weigh(n, src, peak, total):
         b = n // STEPS
         step = n % STEPS
-        s = src[...]
-        column = s.max(axis=0, keepdims=True)
+        s = src[:W1, :]
+        column = src[W1 : W1 + 1, :]
         new = peak
         for u in range(UNIT):
             new = jnp.maximum(new, column[:, u * DH : (u + 1) * DH])
@@ -220,7 +225,7 @@
     second = {}
     for d in range(1, back + 1):
         first[d].wait_recv()
-        for k in range(1, nh):
+        for k in [j for j in FAR_FIRST if j < nh]:
             second[d, k] = remote(
                 slot(d, e), slot(d, e), send2.at[d - 1, k - 1], recv2.at[d - 1, k - 1], c, head_peer(k)
             )
@@ -338,8 +343,8 @@
         pltpu.VMEM((BLOCKS + 1, DH, DH), full),
         pltpu.VMEM((DH, 2 * DH), full),
         pltpu.VMEM((W2, BLOCKS, DH, DH), full),
-        pltpu.VMEM((W1, UNIT * DH), full),
-        pltpu.VMEM((W1, UNIT * DH), full),
+        pltpu.VMEM((W1 + 8, UNIT * DH), full),
+        pltpu.VMEM((W1 + 8, UNIT * DH), full),
         pltpu.VMEM((DH, DH), full),
         pltpu.VMEM((QB, nh * feats), full),
         pltpu.VMEM((BLOCKS, QB, nh * feats), half),

time: 50.4 us -> 50.2 us (level)
  no operation moved by 1% of the time
where the time goes in v7:
time: 50.2 us; the launch traced here: 50 us
  Pallas kernels  48.5 us (97%)
  local copies, waits for them, and re-layouts  1.57 us (3%)
    pallas_call x1, Pallas kernels, body(): pl.pallas_call(kernel, out_shape=jax.ShapeDtypeStruct((rows, feats), half...  48.5 us
    transpose x1, local copies, waits for them, and re-layouts, body(): return stored.T  1.57 us

profile of v7, /device:TPU:1, one launch (start us, length us, event | category | flops | bytes accessed | tf_op | source)
XLA Modules:
  0.0 50.0 jit_solution(18162559847665077931)
XLA Ops:
  0.0 48.5 %shard_map.55 = bf16[128,256]{1,0:T(8,128)(2,1)} custom-call(s32[256]{0:T(256)} %start_ref.1, s32[256]{0:T(256)} %dest_ref.1, bf16[128,512]{1,0:T(8,128)(2,1)} %q_hbm.1, bf16[128,512]{1,0:T(8,128)(2,1)} %kv_hbm.1, bf16[512,2048]{1,0:T(8,128)(2,1)} %w_hbm.1), custom_call_target="tpu_custom_call" | custom-call | tf_op jit(solution)/shard_map/pallas_call | solution.py:366
  48.5 1.6 %copy.6 = bf16[256,128]{1,0:T(8,128)(2,1)} copy(bf16[256,128]{0,1:T(8,128)(2,1)} %bitcast.1) | data formatting | bytes 131072 | tf_op jit(solution)/shard_map/transpose | solution.py:376
